TPU v7x, 32 devices: a whole 2x2x4 slice. The times are simulated.
32 devices in a mesh: plane: 4 (over z), tile: 8 (over y, x, core).
Axes of the slice: x: 2, y: 2, z: 4, core: 2. Of those that a mesh axis runs over, the one named last changes fastest.
Arguments:
- block_dest: int32 [4, 512, 1], P('plane', 'tile'), may hold values from 0 to 7; in each aligned block of 64 rows (0 to 63, 64 to 127, ..., all dimensions but the last counted through in order) at most 16 rows name the same one
- particle_cell: int32 [4, 512, 128], P('plane', 'tile'), may hold values from 0 to 32767, as said below
- particle_offset: float32 [4, 2, 512, 128], P('plane', None, 'tile'), may hold values from 0 to 1
- particle_mass: float32 [4, 512, 128], P('plane', 'tile'), may hold values from -6.7 to 6.7
- ray_cell: int32 [4, 16384], P(None, 'tile'), may hold values from 0 to 32767
- ray_offset: float32 [2, 4, 16384], P(None, None, 'tile'), may hold values from 0 to 1
Outputs:
- lens_fields: float32 [4, 5, 512, 512], P('plane', None, 'tile')
- ray_maps: float32 [4, 4, 6, 16384], P('plane', None, None, 'tile')
Inputs may be any that keep to these rules, and one draw needn't show every extreme that they name: `block_dest`: among the blocks of one device (aligned runs of 64 rows), at most 16 name the same tile, and in every draw some device names some tile exactly 16 times. `particle_cell`: Row-major cell index within the 64 x 512 cells of the block's tile. `ray_cell`: Row-major cell index within the 64 x 512 cells of the ray's own tile.
All inputs are finite; a program needn't handle non-finite values.
Results may differ from a plain program's by a relative error of at most 0.0003.
Values sent between devices are 32-bit elements; how exact they have to be, the bound alone decides.
No kernel may reach another device: no remote copies, remote signals or barrier semaphores. Data moves between devices by JAX's collectives and lax.ppermute only.
A program may use at most 64 MiB of HBM per device.

v0:
```python
import math

import jax
import jax.numpy as jnp
from jax import lax
from jax.sharding import PartitionSpec as P

NG = 512
NP = 1024
BLOCKS_DEV = 64


LENS_WEIGHT = 0.15
SCREEN_SCALE = 0.5
HIGHEST_PRECISION = lax.Precision.HIGHEST


def passed_along(shard, axis, by):
    count = lax.axis_size(axis)
    pairs = [(i, i + by) for i in range(count) if 0 <= i + by < count]
    return lax.ppermute(shard, axis, pairs)


def extended(shard, sides, width):
    for axis, dim in sides:
        count, length = (lax.axis_size(axis), shard.shape[dim])
        up = [(i, (i + 1) % count) for i in range(count - 1)]
        down = [(j, i) for i, j in up]
        last = lax.slice_in_dim(shard, length - width, length, axis=dim)
        first = lax.slice_in_dim(shard, 0, width, axis=dim)
        before = lax.ppermute(last, axis, up)
        after = lax.ppermute(first, axis, down)
        shard = jnp.concatenate([before, shard, after], axis=dim)
    return shard


def trig_tables(count, length):
    index_n = lax.broadcasted_iota(jnp.int32, (count, length), 0)
    index_k = lax.broadcasted_iota(jnp.int32, (count, length), 1)
    phase = (index_n * index_k % length).astype(jnp.float32) * (2.0 * math.pi / length)
    return (jnp.cos(phase), jnp.sin(phase))


def signed_wave(counter, length):
    signed = jnp.where(counter < length // 2, counter, counter - length)
    return signed.astype(jnp.float32) * (2.0 * math.pi / length)


def hat_weights(index_grid, ids, fracs):
    return jnp.where(index_grid == ids[None, :], 1.0 - fracs[None, :], 0.0) + jnp.where(
        index_grid == ids[None, :] + 1, fracs[None, :], 0.0
    )


def deposit(row_ids, row_frac, col_ids, col_frac, weights, row_count, col_count):
    row_iota = lax.broadcasted_iota(jnp.int32, (row_count, 1), 0)
    col_iota = lax.broadcasted_iota(jnp.int32, (col_count, 1), 0)

    def accumulate(total, inputs):
        ids_r, frac_r, ids_c, frac_c, weight_now = inputs
        row_weights = hat_weights(row_iota, ids_r, frac_r) * weight_now[None, :]
        col_weights = hat_weights(col_iota, ids_c, frac_c)
        addition = lax.dot_general(
            row_weights,
            col_weights,
            (((1,), (1,)), ((), ())),
            precision=HIGHEST_PRECISION,
            preferred_element_type=jnp.float32,
        )
        return (total + addition, None)

    total, _ = lax.scan(
        accumulate,
        jnp.zeros((row_count, col_count), jnp.float32),
        (row_ids, row_frac, col_ids, col_frac, weights),
    )
    return total


def interpolate(window, row_anchor, row_pos, col_pos):
    row_floor = jnp.floor(row_pos)
    col_floor = jnp.floor(col_pos)
    frac_row = row_pos - row_floor
    frac_col = col_pos - col_floor
    row_ids = row_floor.astype(jnp.int32) - row_anchor
    col_ids = col_floor.astype(jnp.int32)
    row_iota = lax.broadcasted_iota(jnp.int32, (window.shape[1], 1), 0)
    col_iota = lax.broadcasted_iota(jnp.int32, (window.shape[2], 1), 0)
    row_weights = hat_weights(row_iota, row_ids, frac_row)
    col_weights = hat_weights(col_iota, col_ids, frac_col)
    along_cols = jnp.einsum(
        "frc,cq->frq",
        window,
        col_weights,
        precision=HIGHEST_PRECISION,
        preferred_element_type=jnp.float32,
    )
    return jnp.sum(along_cols * row_weights[None, :, :], axis=1)


def update_state(state, values):
    hess_xx = values[2]
    hess_xy = values[3]
    hess_yy = values[4]
    dist_xx = state[2]
    dist_xy = state[3]
    dist_yx = state[4]
    dist_yy = state[5]
    return jnp.stack(
        [
            state[0] - LENS_WEIGHT * values[0],
            state[1] - LENS_WEIGHT * values[1],
            dist_xx - LENS_WEIGHT * (hess_xx * dist_xx + hess_xy * dist_yx),
            dist_xy - LENS_WEIGHT * (hess_xx * dist_xy + hess_xy * dist_yy),
            dist_yx - LENS_WEIGHT * (hess_xy * dist_xx + hess_yy * dist_yx),
            dist_yy - LENS_WEIGHT * (hess_xy * dist_xy + hess_yy * dist_yy),
        ]
    )


def advance(state, base_row, base_col, window, row_anchor, span):
    row_pos = base_row + span * jnp.tanh(state[0] / span)
    col_pos = base_col + span * jnp.tanh(state[1] / span)
    return update_state(state, interpolate(window, row_anchor, row_pos, col_pos))


def per_device(block_dest, particle_cell, particle_offset, particle_mass, ray_cell, ray_offset):
    tiles = lax.axis_size("tile")
    tile_rows = NG // tiles
    tile_now = lax.axis_index("tile")
    blocks = particle_cell.shape[1]
    block_len = particle_cell.shape[2]
    targets = block_dest[0, :, 0]
    cell_ids = particle_cell[0]
    frac_row = particle_offset[0, 0]
    frac_col = particle_offset[0, 1]
    masses = particle_mass[0]
    scaling = math.sqrt(tile_rows * NG / (BLOCKS_DEV * block_len))
    capacity = 2 * blocks // tiles
    slot_count = capacity * tiles
    chosen = (targets[:, None] == lax.broadcasted_iota(jnp.int32, (1, tiles), 1)).astype(jnp.int32)
    before = jnp.cumsum(chosen, axis=0) - chosen
    ranks = jnp.sum(before * chosen, axis=1)
    slot_ids = targets * capacity + ranks
    slot_map = (lax.broadcasted_iota(jnp.int32, (slot_count, 1), 0) == slot_ids[None, :]).astype(
        jnp.float32
    )
    payload = jnp.stack([cell_ids.astype(jnp.float32), frac_row, frac_col, masses], axis=1)
    payload = payload.reshape(blocks, 4 * block_len)
    outgoing = jnp.dot(
        slot_map, payload, precision=HIGHEST_PRECISION, preferred_element_type=jnp.float32
    ).reshape(slot_count, 4, block_len)
    incoming = lax.all_to_all(outgoing, "tile", split_axis=0, concat_axis=0, tiled=True)
    in_cells = incoming[:, 0].astype(jnp.int32)
    slot_groups = slot_count // 8
    canvas = deposit(
        (in_cells // NG).reshape(slot_groups, -1),
        incoming[:, 1].reshape(slot_groups, -1),
        (in_cells % NG).reshape(slot_groups, -1),
        incoming[:, 2].reshape(slot_groups, -1),
        incoming[:, 3].reshape(slot_groups, -1),
        tile_rows + 1,
        NG,
    )
    spill_row = passed_along(canvas[tile_rows], "tile", 1)
    density = jnp.concatenate([canvas[:1] + spill_row[None, :], canvas[1:tile_rows]], axis=0)
    density = density * scaling
    cos_table, sin_table = trig_tables(NG, NP)
    spec_re = jnp.einsum("ck,rc->kr", cos_table, density, precision=HIGHEST_PRECISION)
    spec_im = -jnp.einsum("ck,rc->kr", sin_table, density, precision=HIGHEST_PRECISION)
    columns = lax.all_to_all(
        jnp.stack([spec_re, spec_im]), "tile", split_axis=1, concat_axis=2, tiled=True
    )
    part_re = columns[0]
    part_im = columns[1]
    full_re = jnp.dot(part_re, cos_table, precision=HIGHEST_PRECISION) + jnp.dot(
        part_im, sin_table, precision=HIGHEST_PRECISION
    )
    full_im = jnp.dot(part_im, cos_table, precision=HIGHEST_PRECISION) - jnp.dot(
        part_re, sin_table, precision=HIGHEST_PRECISION
    )
    freq_count = full_re.shape[0]
    wave_x = signed_wave(lax.broadcasted_iota(jnp.int32, (1, NP), 1), NP)
    wave_y = signed_wave(
        tile_now * freq_count + lax.broadcasted_iota(jnp.int32, (freq_count, 1), 0), NP
    )
    screen = (SCREEN_SCALE * 2.0 * math.pi / NP) ** 2
    factor = -2.0 / (wave_x * wave_x + wave_y * wave_y + screen)
    pot_re = full_re * factor
    pot_im = full_im * factor
    spectra_re = jnp.stack(
        [
            -wave_x * pot_im,
            -wave_y * pot_im,
            -wave_x * wave_x * pot_re,
            -wave_x * wave_y * pot_re,
            -wave_y * wave_y * pot_re,
        ]
    )
    spectra_im = jnp.stack(
        [
            wave_x * pot_re,
            wave_y * pot_re,
            -wave_x * wave_x * pot_im,
            -wave_x * wave_y * pot_im,
            -wave_y * wave_y * pot_im,
        ]
    )
    rows_re = jnp.einsum(
        "fjk,nk->fjn", spectra_re, cos_table, precision=HIGHEST_PRECISION
    ) - jnp.einsum("fjk,nk->fjn", spectra_im, sin_table, precision=HIGHEST_PRECISION)
    rows_im = jnp.einsum(
        "fjk,nk->fjn", spectra_im, cos_table, precision=HIGHEST_PRECISION
    ) + jnp.einsum("fjk,nk->fjn", spectra_re, sin_table, precision=HIGHEST_PRECISION)
    returned = lax.all_to_all(
        jnp.stack([rows_re, rows_im], axis=1), "tile", split_axis=3, concat_axis=2, tiled=True
    )
    fields = (
        jnp.einsum("fjr,cj->frc", returned[:, 0], cos_table, precision=HIGHEST_PRECISION)
        - jnp.einsum("fjr,cj->frc", returned[:, 1], sin_table, precision=HIGHEST_PRECISION)
    ) / float(NP * NP)
    window = extended(fields, (("tile", 1),), tile_rows)
    row_anchor = (tile_now - 1) * tile_rows
    base_row = (tile_now * tile_rows + ray_cell // NG).astype(jnp.float32) + ray_offset[0]
    base_col = (ray_cell % NG).astype(jnp.float32) + ray_offset[1]
    span = float(tile_rows - 1)
    plane_now = lax.axis_index("plane")
    planes = lax.axis_size("plane")
    batches = ray_cell.shape[0]
    rays = ray_cell.shape[1]
    unit_state = jnp.array([0.0, 0.0, 1.0, 0.0, 0.0, 1.0], jnp.float32)[:, None]
    start_state = jnp.broadcast_to(unit_state, (6, rays))

    def batch_turn(turn_index, carry):
        inbox, result = carry
        batch_index = turn_index - plane_now
        active = (batch_index >= 0) & (batch_index < batches)
        clipped = jnp.clip(batch_index, 0, batches - 1)
        current = jnp.where(plane_now == 0, start_state, inbox)
        rows_now = lax.dynamic_index_in_dim(base_row, clipped, 0, keepdims=False)
        cols_now = lax.dynamic_index_in_dim(base_col, clipped, 0, keepdims=False)
        moved = advance(current, rows_now, cols_now, window, row_anchor, span)
        previous = lax.dynamic_index_in_dim(result, clipped, 0, keepdims=False)
        result = lax.dynamic_update_index_in_dim(
            result, jnp.where(active, moved, previous), clipped, 0
        )
        inbox = passed_along(moved, "plane", 1)
        return (inbox, result)

    _, ray_maps = lax.fori_loop(
        0,
        batches + planes - 1,
        batch_turn,
        (start_state, jnp.zeros((batches, 6, rays), jnp.float32)),
    )
    return (fields[None], ray_maps[None])


def solution(mesh):
    return jax.shard_map(
        per_device,
        mesh=mesh,
        in_specs=(
            P("plane", "tile", None),
            P("plane", "tile", None),
            P("plane", None, "tile", None),
            P("plane", "tile", None),
            P(None, "tile"),
            P(None, None, "tile"),
        ),
        out_specs=(P("plane", None, "tile", None), P("plane", None, None, "tile")),
        check_vma=False,
    )
```

profile of v0, /device:TPU:26, one launch (start us, length us, event | category | flops | bytes accessed | tf_op | source)
XLA Modules:
  0.0 429.1 jit_solution(7401390829059903527)
XLA Ops:
  6.5 4.3 all-to-all-start
  10.8 5.4 %all-to-all-done = f32[128,4,128]{2,1,0:T(4,128)S(1)} async-done(((f32[128,4,128]{2,1,0:T(4,128)}), f32[128,4,128]{2,1,0:T(4,128)S(1)}, u32[]{:S(2)}, u32[]{:S(2)}) %all-to-all-start) | async-done | bytes 262176 | tf_op jit(solution)/shard_map/all_to_all | solution.py:153
  17.1 41.6 %while.30 = (s32[]{:T(128)}, f32[65,512]{1,0:T(8,128)S(1)}, s32[16,1024]{1,0:T(8,128)S(1)}, f32[16,1024]{1,0:T(8,128)S(1)}, f32[16,1024]{1,0:T(8,128)S(1)}, /*in...) while((s32[]{:T(128)}, f32[65,512]{1,0:T(8,128)S(1)}, ...), condition=%wide.region_3.4_spmd.clone.clone, body=%wide.region_2.3_spmd.clone.clone.sunk | while | flops 412036096 | bytes 360563 | solution.py:72
  19.8 2.5 fusion.206
  22.4 2.5 fusion.206
  25.0 2.5 fusion.206
  27.6 2.5 fusion.206
  30.2 2.5 fusion.206
  32.8 2.5 fusion.206
  38.0 2.5 fusion.206
  43.2 2.5 fusion.206
  48.4 2.5 fusion.206
  53.6 2.5 fusion.206
  60.7 2.9 collective-permute-done.1
  63.6 9.6 %convolution_bitcast_fusion = f32[1,1024,64]{1,2,0:T(8,128)S(1)} fusion(f32[63,512]{1,0:T(8,128)S(1)} %slice.145, f32[1,512]{1,0:T(1,128)S(1)} %slice_add_fusion), kind=kOutput, calls=%fused_computation.113 | convolution fusion | flops 410058752 | bytes 393216 | tf_op jit(solution)/shard_map/ck,rc->kr/dot_general | solution.py:169
  73.2 9.7 %fusion.82 = f32[1,1024,64]{1,2,0:T(8,128)S(1)} fusion(f32[63,512]{1,0:T(8,128)S(1)} %slice.145, f32[1,512]{1,0:T(1,128)S(1)} %slice_add_fusion), kind=kOutput, calls=%fused_computation.112 | convolution fusion | flops 410124288 | bytes 393216 | tf_op jit(solution)/shard_map/ck,rc->kr/dot_general | solution.py:170
  85.4 4.7 %all-to-all-start.1 = ((f32[8,1,16384]{2,1,0:T(1,128)}), f32[8,1,16384]{2,1,0:T(1,128)S(1)}, u32[]{:S(2)}, u32[]{:S(2)}) async-start(f32[8,1,16384]{2,1,0:T(1,128)} %reshape.237), calls=%async_computation.1 | async-start | bytes 1048576 | tf_op jit(solution)/shard_map/all_to_all | solution.py:171
  90.2 8.1 %all-to-all-done.1 = f32[8,1,16384]{2,1,0:T(1,128)S(1)} async-done(((f32[8,1,16384]{2,1,0:T(1,128)}), f32[8,1,16384]{2,1,0:T(1,128)S(1)}, u32[]{:S(2)}, u32[]{:S(2)}) %all-to-all-start.1) | async-done | bytes 524320 | tf_op jit(solution)/shard_map/all_to_all | solution.py:171
  102.0 10.0 %fusion.88 = f32[128,1024]{1,0:T(8,128)S(1)} fusion(f32[128,512]{0,1:T(8,128)S(1)} %bitcast.227), kind=kOutput, calls=%fused_computation.116 | convolution fusion | flops 812646400 | bytes 786432 | tf_op jit(solution)/shard_map/dot_general | solution.py:176
  112.1 10.0 %fusion.90 = f32[128,1024]{1,0:T(8,128)S(1)} fusion(f32[128,512]{0,1:T(8,128)S(1)} %bitcast.229), kind=kOutput, calls=%fused_computation.117 | convolution fusion | flops 812646400 | bytes 786432 | tf_op jit(solution)/shard_map/dot_general | solution.py:179
  122.1 10.3 %bitcast_dynamic-update-slice_fusion.3 = (f32[5,128,1024]{2,1,0:T(8,128)S(1)}, f32[128,1024]{1,0:T(8,128)S(1)}) fusion(f32[1024]{0:T(1024)S(1)} %get-tuple-element.419, f32[128]{0:T(128)S(1)} %get-tuple-element.418, f32[1024]{0:T(1024)S(1)} %get-tuple-element.420, f32[128,1024]{1,0:T(8,128)S(1)} %fusion.88, f32[128,512]{0,1:T(8,128)S(1)} %bitcast.230), kind=kOutput, calls=%fused_computation.128 | convolution fusion | flops 813432832 | bytes 1843712 | tf_op jit(solution)/shard_map/dot_general | solution.py:176
  132.5 10.2 %bitcast_dynamic-update-slice_fusion.1 = (f32[5,128,1024]{2,1,0:T(8,128)S(1)}, f32[128,1024]{1,0:T(8,128)S(1)}) fusion(f32[5,128,1024]{2,1,0:T(8,128)S(1)} %bitcast_dynamic-update-slice_fusion.2, f32[1024]{0:T(1024)S(1)} %fusion.123, f32[128]{0:T(128)S(1)} %get-tuple-element.418, f32[1024]{0:T(1024)S(1)} %get-tuple-element.420, ...), kind=kOutput, calls=%fused_computation.126 | convolution fusion | flops 813432832 | bytes 1843712 | tf_op jit(solution)/shard_map/dot_general | solution.py:179
  143.2 12.7 %fusion.51 = f32[5,128,512]{2,1,0:T(8,128)S(1)} fusion(f32[5,128,1024]{2,1,0:T(8,128)S(1)} %get-tuple-element.401), kind=kOutput, calls=%fused_computation.87 | convolution fusion | flops 4033871872 | bytes 3932160 | tf_op jit(solution)/shard_map/fjk,nk->fjn/dot_general | solution.py:211
  155.9 12.9 %fusion.49 = f32[5,128,512]{2,1,0:T(8,128)S(1)} fusion(f32[5,128,1024]{2,1,0:T(8,128)S(1)} %bitcast_dynamic-update-slice_fusion.4), kind=kOutput, calls=%fused_computation.85 | convolution fusion | flops 4033871872 | bytes 3932160 | tf_op jit(solution)/shard_map/fjk,nk->fjn/dot_general | solution.py:214
  168.8 12.8 %fusion.65 = f32[5,1,128,512]{3,2,0,1:T(8,128)S(1)} fusion(f32[5,128,512]{2,1,0:T(8,128)S(1)} %fusion.51, f32[5,128,1024]{2,1,0:T(8,128)S(1)} %bitcast_dynamic-update-slice_fusion.4), kind=kOutput, calls=%fused_computation.100 | convolution fusion | flops 4034199552 | bytes 5242880 | tf_op jit(solution)/shard_map/fjk,nk->fjn/dot_general | solution.py:209
  181.6 13.0 %fusion.71 = f32[5,1,128,512]{3,2,0,1:T(8,128)S(1)} fusion(f32[5,128,512]{2,1,0:T(8,128)S(1)} %fusion.49, f32[5,128,1024]{2,1,0:T(8,128)S(1)} %get-tuple-element.401), kind=kOutput, calls=%fused_computation.102 | convolution fusion | flops 4034199552 | bytes 5242880 | tf_op jit(solution)/shard_map/fjk,nk->fjn/dot_general | solution.py:212
  194.9 3.2 copy.43
  198.2 35.7 %all_to_all.38 = f32[5,2,128,512]{2,1,0,3:T(2,128)S(1)} all-to-all(f32[5,2,128,512]{2,1,0,3:T(2,128)} %copy.43), channel_id=1, replica_groups=mesh['plane'=4,'tile'=8] {'tile'}, dimensions={3} | all-to-all | bytes 5242880 | tf_op jit(solution)/shard_map/all_to_all | solution.py:215
  237.6 11.5 %fusion.47 = f32[5,64,512]{2,1,0:T(8,128)S(1)} fusion(f32[5,2,1024,64]{2,3,0,1:T(8,128)} %all_to_all.34), kind=kOutput, calls=%fused_computation.83 | convolution fusion | flops 2020605952 | bytes 1966080 | tf_op jit(solution)/shard_map/fjr,cj->frc/dot_general | solution.py:220
  249.2 10.2 %fusion.77 = f32[5,64,512]{2,1,0:T(8,128)S(1)} fusion(f32[5,64,512]{2,1,0:T(8,128)S(1)} %fusion.47, f32[5,2,1024,64]{2,3,0,1:T(8,128)S(1)} %copy-done), kind=kOutput, calls=%fused_computation.106 | convolution fusion | flops 2020933632 | bytes 2621440 | tf_op jit(solution)/shard_map/fjr,cj->frc/dot_general | solution.py:219
  261.3 3.6 collective-permute-start.3
  265.7 5.6 %collective-permute-done.2 = f32[5,64,512]{2,1,0:T(8,128)S(1)} collective-permute-done((f32[5,64,512]{2,1,0:T(8,128)S(1)}, f32[5,64,512]{2,1,0:T(8,128)S(1)}, u32[]{:S(2)}, u32[]{:S(2)}) %collective-permute-start.2) | collective-permute-done | bytes 655392 | tf_op jit(solution)/shard_map/ppermute | solution.py:31
  271.3 6.0 %collective-permute-done.3 = f32[5,64,512]{2,1,0:T(8,128)} collective-permute-done((f32[5,64,512]{2,1,0:T(8,128)S(1)}, f32[5,64,512]{2,1,0:T(8,128)}, u32[]{:S(2)}, u32[]{:S(2)}) %collective-permute-start.3) | collective-permute-done | bytes 655392 | tf_op jit(solution)/shard_map/ppermute | solution.py:32
  278.7 149.2 %while.29 = (s32[]{:T(128)}, f32[6,2048]{1,0:T(8,128)S(1)}, f32[4,6,2048]{2,0,1:T(4,128)S(1)}, pred[]{:T(512)}, s32[]{:T(128)}, /*index=5*/f32[4,2048]{1,0:T(4,1...) while((s32[]{:T(128)}, f32[6,2048]{1,0:T(8,128)S(1)}, ...), condition=%wide.region_6.7_spmd.clone, body=%wide.region_4.6_spmd.sunk.clone.sunk | while | flops 12090847232 | bytes 6439184 | solution.py:250
  280.2 13.6 %fusion.202 = f32[5,2048]{1,0:T(8,128)S(1)} fusion(f32[192,2048]{1,0:T(8,128)S(1)} %select_add_fusion.2, f32[5,192,512]{2,1,0:T(8,128)S(1)} %get-tuple-element.626, f32[2048]{0:T(1024)S(1)} %bitcast.232, s32[2048]{0:T(1024)S(1)} %bitcast.233, f32[2048]{0:T(1024)S(1)} %bitcast.231, s32[2048]{0:T(1024)S(1)} %bitcast.234), kind=kOutput, calls=%fused_computation.3.clone.1 | convolution fusion | flops 12088760320 | bytes 3612672 | tf_op jit(solution)/shard_map/while/body/eval_jaxpr/frc,cq->frq/dot_general | solution.py:91
  296.6 4.2 collective-permute-done
  302.1 13.6 %fusion.202 = f32[5,2048]{1,0:T(8,128)S(1)} fusion(f32[192,2048]{1,0:T(8,128)S(1)} %select_add_fusion.2, f32[5,192,512]{2,1,0:T(8,128)S(1)} %get-tuple-element.626, f32[2048]{0:T(1024)S(1)} %bitcast.232, s32[2048]{0:T(1024)S(1)} %bitcast.233, f32[2048]{0:T(1024)S(1)} %bitcast.231, s32[2048]{0:T(1024)S(1)} %bitcast.234), kind=kOutput, calls=%fused_computation.3.clone.1 | convolution fusion | flops 12088760320 | bytes 3612672 | tf_op jit(solution)/shard_map/while/body/eval_jaxpr/frc,cq->frq/dot_general | solution.py:91
  318.5 3.5 collective-permute-done
  323.3 13.6 %fusion.202 = f32[5,2048]{1,0:T(8,128)S(1)} fusion(f32[192,2048]{1,0:T(8,128)S(1)} %select_add_fusion.2, f32[5,192,512]{2,1,0:T(8,128)S(1)} %get-tuple-element.626, f32[2048]{0:T(1024)S(1)} %bitcast.232, s32[2048]{0:T(1024)S(1)} %bitcast.233, f32[2048]{0:T(1024)S(1)} %bitcast.231, s32[2048]{0:T(1024)S(1)} %bitcast.234), kind=kOutput, calls=%fused_computation.3.clone.1 | convolution fusion | flops 12088760320 | bytes 3612672 | tf_op jit(solution)/shard_map/while/body/eval_jaxpr/frc,cq->frq/dot_general | solution.py:91
  339.7 3.5 collective-permute-done
  344.5 13.6 %fusion.202 = f32[5,2048]{1,0:T(8,128)S(1)} fusion(f32[192,2048]{1,0:T(8,128)S(1)} %select_add_fusion.2, f32[5,192,512]{2,1,0:T(8,128)S(1)} %get-tuple-element.626, f32[2048]{0:T(1024)S(1)} %bitcast.232, s32[2048]{0:T(1024)S(1)} %bitcast.233, f32[2048]{0:T(1024)S(1)} %bitcast.231, s32[2048]{0:T(1024)S(1)} %bitcast.234), kind=kOutput, calls=%fused_computation.3.clone.1 | convolution fusion | flops 12088760320 | bytes 3612672 | tf_op jit(solution)/shard_map/while/body/eval_jaxpr/frc,cq->frq/dot_general | solution.py:91
  360.9 3.5 collective-permute-done
  365.6 13.6 %fusion.202 = f32[5,2048]{1,0:T(8,128)S(1)} fusion(f32[192,2048]{1,0:T(8,128)S(1)} %select_add_fusion.2, f32[5,192,512]{2,1,0:T(8,128)S(1)} %get-tuple-element.626, f32[2048]{0:T(1024)S(1)} %bitcast.232, s32[2048]{0:T(1024)S(1)} %bitcast.233, f32[2048]{0:T(1024)S(1)} %bitcast.231, s32[2048]{0:T(1024)S(1)} %bitcast.234), kind=kOutput, calls=%fused_computation.3.clone.1 | convolution fusion | flops 12088760320 | bytes 3612672 | tf_op jit(solution)/shard_map/while/body/eval_jaxpr/frc,cq->frq/dot_general | solution.py:91
  382.0 3.5 collective-permute-done
  386.8 13.6 %fusion.202 = f32[5,2048]{1,0:T(8,128)S(1)} fusion(f32[192,2048]{1,0:T(8,128)S(1)} %select_add_fusion.2, f32[5,192,512]{2,1,0:T(8,128)S(1)} %get-tuple-element.626, f32[2048]{0:T(1024)S(1)} %bitcast.232, s32[2048]{0:T(1024)S(1)} %bitcast.233, f32[2048]{0:T(1024)S(1)} %bitcast.231, s32[2048]{0:T(1024)S(1)} %bitcast.234), kind=kOutput, calls=%fused_computation.3.clone.1 | convolution fusion | flops 12088760320 | bytes 3612672 | tf_op jit(solution)/shard_map/while/body/eval_jaxpr/frc,cq->frq/dot_general | solution.py:91
  403.2 3.5 collective-permute-done
  408.0 13.6 %fusion.202 = f32[5,2048]{1,0:T(8,128)S(1)} fusion(f32[192,2048]{1,0:T(8,128)S(1)} %select_add_fusion.2, f32[5,192,512]{2,1,0:T(8,128)S(1)} %get-tuple-element.626, f32[2048]{0:T(1024)S(1)} %bitcast.232, s32[2048]{0:T(1024)S(1)} %bitcast.233, f32[2048]{0:T(1024)S(1)} %bitcast.231, s32[2048]{0:T(1024)S(1)} %bitcast.234), kind=kOutput, calls=%fused_computation.3.clone.1 | convolution fusion | flops 12088760320 | bytes 3612672 | tf_op jit(solution)/shard_map/while/body/eval_jaxpr/frc,cq->frq/dot_general | solution.py:91
  424.4 3.5 collective-permute-done
  (214 shorter events, 67.6 us)
Async XLA Ops:
  6.5 9.7 %all-to-all-start = ((f32[128,4,128]{2,1,0:T(4,128)}), f32[128,4,128]{2,1,0:T(4,128)S(1)}, u32[]{:S(2)}, u32[]{:S(2)}) async-start(f32[128,4,128]{2,1,0:T(4,128)} %copy.38), calls=%async_computation | async-start | bytes 524288 | tf_op jit(solution)/shard_map/all_to_all | solution.py:153
  58.7 4.9 %collective-permute-start.1 = (f32[512]{0:T(512)S(1)}, f32[512]{0:T(512)S(1)}, u32[]{:S(2)}, u32[]{:S(2)}) collective-permute-start(f32[512]{0:T(512)S(1)} %bitcast.248), channel_id=1, source_target_pairs={{0,1},{1,2},{2,3},{3,4},{4,5},{5,6},{6,7},{8,9},{9,10},{10,11},{11... | collective-permute-start | bytes 6152 | tf_op jit(solution)/shard_map/ppermute | solution.py:21
  85.4 12.9 %all-to-all-start.1 = ((f32[8,1,16384]{2,1,0:T(1,128)}), f32[8,1,16384]{2,1,0:T(1,128)S(1)}, u32[]{:S(2)}, u32[]{:S(2)}) async-start(f32[8,1,16384]{2,1,0:T(1,128)} %reshape.237), calls=%async_computation.1 | async-start | bytes 1048576 | tf_op jit(solution)/shard_map/all_to_all | solution.py:171
  237.6 11.5 %copy-start = (f32[5,2,1024,64]{2,3,0,1:T(8,128)S(1)}, f32[5,2,1024,64]{2,3,0,1:T(8,128)}, u32[]{:S(2)}) copy-start(f32[5,2,1024,64]{2,3,0,1:T(8,128)} %all_to_all.34) | copy-start | bytes 7864324
  249.1 15.8 %copy-start.3 = (f32[2,4,2048]{2,1,0:T(4,128)S(1)}, f32[2,4,2048]{2,1,0:T(4,128)}, u32[]{:S(2)}) copy-start(f32[2,4,2048]{2,1,0:T(4,128)} %param.16) | copy-start | bytes 196612
  249.1 15.8 %copy-start.4 = (s32[4,2048]{1,0:T(4,128)S(1)}, s32[4,2048]{1,0:T(4,128)}, u32[]{:S(2)}) copy-start(s32[4,2048]{1,0:T(4,128)} %param.15) | copy-start | bytes 98308
  259.4 19.3 %copy-start.2 = (f32[5,64,512]{2,1,0:T(8,128)}, f32[5,64,512]{2,1,0:T(8,128)S(1)}, u32[]{:S(2)}) copy-start(f32[5,64,512]{2,1,0:T(8,128)S(1)} %fusion.77) | copy-start | bytes 1966084
  259.4 11.9 %collective-permute-start.2 = (f32[5,64,512]{2,1,0:T(8,128)S(1)}, f32[5,64,512]{2,1,0:T(8,128)S(1)}, u32[]{:S(2)}, u32[]{:S(2)}) collective-permute-start(f32[5,64,512]{2,1,0:T(8,128)S(1)} %fusion.77), channel_id=1, source_target_pairs={{0,1},{1,2},{2,3},{3,4},{4,5},{5,6},{6,7},{8,9},{9,10},{10,11},{11... | collective-permute-start | bytes 1966088 | tf_op jit(solution)/shard_map/ppermute | solution.py:31
  261.3 16.0 %collective-permute-start.3 = (f32[5,64,512]{2,1,0:T(8,128)S(1)}, f32[5,64,512]{2,1,0:T(8,128)}, u32[]{:S(2)}, u32[]{:S(2)}) collective-permute-start(f32[5,64,512]{2,1,0:T(8,128)S(1)} %fusion.77), channel_id=1, source_target_pairs={{1,0},{2,1},{3,2},{4,3},{5,4},{6,5},{7,6},{9,8},{10,9},{11,10},{12... | collective-permute-start | bytes 1966088 | tf_op jit(solution)/shard_map/ppermute | solution.py:32
  265.7 13.0 %copy-start.5 = (f32[6]{0:T(128)S(1)}, f32[6]{0:T(128)}, u32[]{:S(2)}) copy-start(f32[6]{0:T(128)} %constant.210.clone) | copy-start | bytes 76
  294.0 6.8 %collective-permute-start = (f32[6,2048]{1,0:T(8,128)S(1)}, f32[6,2048]{1,0:T(8,128)S(1)}, u32[]{:S(2)}, u32[]{:S(2)}) collective-permute-start(f32[6,2048]{1,0:T(8,128)S(1)} %stack.135), channel_id=1, source_target_pairs={{0,8},{8,16},{16,24},{1,9},{9,17},{17,25},{2,10},{10,18},{18,26},{... | collective-permute-start | bytes 147464 | tf_op jit(solution)/shard_map/while/body/eval_jaxpr/ppermute | solution.py:21
  315.9 6.2 %collective-permute-start = (f32[6,2048]{1,0:T(8,128)S(1)}, f32[6,2048]{1,0:T(8,128)S(1)}, u32[]{:S(2)}, u32[]{:S(2)}) collective-permute-start(f32[6,2048]{1,0:T(8,128)S(1)} %stack.135), channel_id=1, source_target_pairs={{0,8},{8,16},{16,24},{1,9},{9,17},{17,25},{2,10},{10,18},{18,26},{... | collective-permute-start | bytes 147464 | tf_op jit(solution)/shard_map/while/body/eval_jaxpr/ppermute | solution.py:21
  337.1 6.2 %collective-permute-start = (f32[6,2048]{1,0:T(8,128)S(1)}, f32[6,2048]{1,0:T(8,128)S(1)}, u32[]{:S(2)}, u32[]{:S(2)}) collective-permute-start(f32[6,2048]{1,0:T(8,128)S(1)} %stack.135), channel_id=1, source_target_pairs={{0,8},{8,16},{16,24},{1,9},{9,17},{17,25},{2,10},{10,18},{18,26},{... | collective-permute-start | bytes 147464 | tf_op jit(solution)/shard_map/while/body/eval_jaxpr/ppermute | solution.py:21
  358.2 6.2 %collective-permute-start = (f32[6,2048]{1,0:T(8,128)S(1)}, f32[6,2048]{1,0:T(8,128)S(1)}, u32[]{:S(2)}, u32[]{:S(2)}) collective-permute-start(f32[6,2048]{1,0:T(8,128)S(1)} %stack.135), channel_id=1, source_target_pairs={{0,8},{8,16},{16,24},{1,9},{9,17},{17,25},{2,10},{10,18},{18,26},{... | collective-permute-start | bytes 147464 | tf_op jit(solution)/shard_map/while/body/eval_jaxpr/ppermute | solution.py:21
  379.4 6.2 %collective-permute-start = (f32[6,2048]{1,0:T(8,128)S(1)}, f32[6,2048]{1,0:T(8,128)S(1)}, u32[]{:S(2)}, u32[]{:S(2)}) collective-permute-start(f32[6,2048]{1,0:T(8,128)S(1)} %stack.135), channel_id=1, source_target_pairs={{0,8},{8,16},{16,24},{1,9},{9,17},{17,25},{2,10},{10,18},{18,26},{... | collective-permute-start | bytes 147464 | tf_op jit(solution)/shard_map/while/body/eval_jaxpr/ppermute | solution.py:21
  400.6 6.2 %collective-permute-start = (f32[6,2048]{1,0:T(8,128)S(1)}, f32[6,2048]{1,0:T(8,128)S(1)}, u32[]{:S(2)}, u32[]{:S(2)}) collective-permute-start(f32[6,2048]{1,0:T(8,128)S(1)} %stack.135), channel_id=1, source_target_pairs={{0,8},{8,16},{16,24},{1,9},{9,17},{17,25},{2,10},{10,18},{18,26},{... | collective-permute-start | bytes 147464 | tf_op jit(solution)/shard_map/while/body/eval_jaxpr/ppermute | solution.py:21
  421.8 6.2 %collective-permute-start = (f32[6,2048]{1,0:T(8,128)S(1)}, f32[6,2048]{1,0:T(8,128)S(1)}, u32[]{:S(2)}, u32[]{:S(2)}) collective-permute-start(f32[6,2048]{1,0:T(8,128)S(1)} %stack.135), channel_id=1, source_target_pairs={{0,8},{8,16},{16,24},{1,9},{9,17},{17,25},{2,10},{10,18},{18,26},{... | collective-permute-start | bytes 147464 | tf_op jit(solution)/shard_map/while/body/eval_jaxpr/ppermute | solution.py:21
  428.0 0.7 copy-start.1
where the time goes:
time: 437 us; the launch traced here: 429 us
  matrix products  269 us (62%)
  waiting for transfers between devices  53.6 us (12%)
  blocking collectives  35.7 us (8%)
  starting transfers between devices  25.5 us (6%)
  local copies, waits for them, and re-layouts  23.8 us (5%)
  other arithmetic  18.1 us (4%)
    dot_general x7, matrix products, interpolate(): jnp.einsum('frc,cq->frq', window, col_weights, precision=HIGHEST_PRECISIO...  95 us
    dot_general x16, matrix products, accumulate(): lax.dot_general(row_weights, col_weights, (((1,), (1,)), ((), ())), preci...  39.9 us
    all_to_all x1, blocking collectives, per_device(): lax.all_to_all(jnp.stack([rows_re, rows_im], axis=1), 'tile', split_axis=...  35.7 us
    ppermute x8, waiting for transfers between devices, passed_along(): return lax.ppermute(shard, axis, pairs)  28.5 us
    dot_general x1, matrix products, per_device(): jnp.einsum('fjk,nk->fjn', spectra_im, cos_table, precision=HIGHEST_PRECIS...  13 us
    dot_general x1, matrix products, per_device(): jnp.einsum('fjk,nk->fjn', spectra_re, sin_table, precision=HIGHEST_PRECIS...  12.9 us
    dot_general x1, matrix products, per_device(): jnp.einsum('fjk,nk->fjn', spectra_re, cos_table, precision=HIGHEST_PRECIS...  12.8 us
    dot_general x1, matrix products, per_device(): jnp.einsum('fjk,nk->fjn', spectra_im, sin_table, precision=HIGHEST_PRECIS...  12.7 us
  transfers between devices with their start and end apart: 12, of which 12 were waited for; matrix products, arithmetic and copies ran while one was open for 2% of the time, Pallas kernels for 0%

commit v1 on v0

v1 whole, which is shorter than its diff:
```python
import math

import jax
import jax.numpy as jnp
import numpy as np
from jax import lax
from jax.experimental import pallas as pl
from jax.experimental.pallas import tpu as pltpu
from jax.sharding import PartitionSpec as P

NG = 512
NP = 2 * NG
HALF = NP // 2
BLOCKS_DEV = 64

LENS_WEIGHT = 0.15
SCREEN_SCALE = 0.5
MU2 = (SCREEN_SCALE * 2.0 * math.pi / NP) ** 2
WAVE = 2.0 * math.pi / NP
F32 = jnp.float32
BF16 = jnp.bfloat16
VMEM = pltpu.VMEM
RAY_CHUNK = 256


def vmem_spec():
    return pl.BlockSpec(memory_space=pltpu.VMEM)


def smem_spec():
    return pl.BlockSpec(memory_space=pltpu.SMEM)


def split(x):
    hi = x.astype(BF16)
    return hi, (x - hi.astype(F32)).astype(BF16)


def dot_nt(a, b):
    return lax.dot_general(a, b, (((1,), (1,)), ((), ())), preferred_element_type=F32)


def dot_nn(a, b):
    return lax.dot_general(a, b, (((1,), (0,)), ((), ())), preferred_element_type=F32)


def route_kernel(dest_ref, cell_ref, offset_ref, mass_ref, out_ref, count_ref):
    tiles = count_ref.shape[0]
    blocks = cell_ref.shape[1]
    cap = out_ref.shape[0] // (4 * tiles)
    out_ref[...] = jnp.zeros(out_ref.shape, F32)
    for t in range(tiles):
        count_ref[t] = 0

    def place(i, carry):
        dest = dest_ref[i]
        rank = count_ref[dest]
        count_ref[dest] = rank + 1
        row = dest * (4 * cap) + rank
        out_ref[pl.ds(row, 1), :] = cell_ref[0, pl.ds(i, 1), :].astype(F32)
        out_ref[pl.ds(row + cap, 1), :] = offset_ref[0, 0, pl.ds(i, 1), :]
        out_ref[pl.ds(row + 2 * cap, 1), :] = offset_ref[0, 1, pl.ds(i, 1), :]
        out_ref[pl.ds(row + 3 * cap, 1), :] = mass_ref[0, pl.ds(i, 1), :]
        return carry

    lax.fori_loop(0, blocks, place, 0)


def deposit_kernel(in_ref, out_ref, acc_ref, *, scaling, tile_rows):
    tiles = in_ref.shape[0]
    cap = in_ref.shape[1] // 4
    lanes = in_ref.shape[2]
    group = min(8, cap)
    rows = -(-(tile_rows + 1) // 16) * 16
    acc_ref[...] = jnp.zeros(acc_ref.shape, F32)
    row_iota = lax.broadcasted_iota(jnp.int32, (rows, lanes), 0).astype(F32).astype(BF16)
    col_iota = (lax.broadcasted_iota(jnp.int32, (NG, lanes), 0) - NG // 2).astype(F32).astype(BF16)
    zero = jnp.zeros((), BF16)
    one = jnp.ones((), BF16)

    def step(src, start):
        pieces_r = []
        pieces_c = []
        for j in range(start, start + group):
            cell = in_ref[src, pl.ds(j, 1), :].astype(jnp.int32)
            frac_r = in_ref[src, pl.ds(cap + j, 1), :]
            frac_c = in_ref[src, pl.ds(2 * cap + j, 1), :]
            mass = in_ref[src, pl.ds(3 * cap + j, 1), :]
            row_id = (cell // NG).astype(F32)
            col_id = (cell % NG - NG // 2).astype(F32).astype(BF16)
            first = row_iota == row_id.astype(BF16)
            second = row_iota == (row_id + 1.0).astype(BF16)
            upper = mass * (1.0 - frac_r)
            lower = mass * frac_r
            rows_now = []
            for side in (1.0 - frac_c, frac_c):
                a_hi, a_lo = split(upper * side)
                b_hi, b_lo = split(lower * side)
                rows_now.append(jnp.where(first, a_hi, jnp.where(second, b_hi, zero)))
                rows_now.append(jnp.where(first, a_lo, jnp.where(second, b_lo, zero)))
            pieces_r.append(jnp.concatenate(rows_now, axis=0))
            pieces_c.append(jnp.where(col_iota == col_id, one, zero))
        acc_ref[...] += dot_nt(jnp.concatenate(pieces_r, axis=1), jnp.concatenate(pieces_c, axis=1))

    def per_source(src, carry):
        step(src, 0)
        for start in range(group, cap, group):
            block = in_ref[src, pl.ds(3 * cap + start, group), :]

            @pl.when(jnp.max(jnp.abs(block)) > 0.0)
            def _():
                step(src, start)

        return carry

    lax.fori_loop(0, tiles, per_source, 0)
    near = acc_ref[0:rows, :] + acc_ref[rows : 2 * rows, :]
    far = acc_ref[2 * rows : 3 * rows, :] + acc_ref[3 * rows : 4 * rows, :]
    lane = lax.broadcasted_iota(jnp.int32, (rows, NG), 1)
    total = (near + jnp.where(lane == 0, 0.0, pltpu.roll(far, 1, 1))) * scaling
    out_ref[...] = total[0 : out_ref.shape[0], :]


def fields_kernel(
    info_ref,
    mine_ref,
    other_ref,
    v_hi_ref,
    v_lo_ref,
    w0_ref,
    phase_ref,
    lens_ref,
    tab_hi_ref,
    tab_lo_ref,
    dens_ref,
    dens_hi_ref,
    dens_lo_ref,
    u_hi_ref,
    u_lo_ref,
    ba_ref,
    l_hi_ref,
    l_lo_ref,
    *,
    tile_rows,
):
    tile = info_ref[0]
    parity = info_ref[1]
    pairs = mine_ref.shape[0]
    tiles = 2 * pairs
    win = 3 * tile_rows
    pad = tile_rows
    zeros = jnp.zeros((pad, NG), F32)
    dens_ref[0:pad, :] = zeros
    dens_ref[pad + NG : pad + NG + pad, :] = zeros
    for half, src in ((0, mine_ref), (1, other_ref)):
        for j in range(pairs):
            t = 2 * j + jnp.bitwise_xor(parity, half)
            row = pl.multiple_of(pad + t * tile_rows, 8)
            dens_ref[pl.ds(row, tile_rows), :] = src[j, 0:tile_rows, :]
    for half, src in ((0, mine_ref), (1, other_ref)):
        for j in range(pairs):
            t = 2 * j + jnp.bitwise_xor(parity, half)
            row = pl.multiple_of(pad + (t + 1) * tile_rows, 8)
            spill = jnp.where(t + 1 < tiles, src[j, tile_rows : tile_rows + 8, :], 0.0)
            dens_ref[pl.ds(row, 8), :] += spill
    d_hi, d_lo = split(dens_ref[pad : pad + NG, :])
    dens_hi_ref[...] = d_hi
    dens_lo_ref[...] = d_lo

    half_lane = lax.broadcasted_iota(jnp.int32, (1, HALF), 1).astype(F32) * WAVE
    w_cos = w0_ref[:, 0:HALF]
    w_sin = w0_ref[:, HALF:NP]
    for rows, cols, value in (
        (0, 0, w_cos),
        (0, HALF, w_sin),
        (win, 0, -half_lane * w_sin),
        (win, HALF, half_lane * w_cos),
    ):
        hi, lo = split(value)
        u_hi_ref[rows : rows + win, cols : cols + HALF] = hi
        u_lo_ref[rows : rows + win, cols : cols + HALF] = lo

    lane = lax.broadcasted_iota(jnp.int32, (1, NP), 1)
    k_slot = jnp.where(lane < HALF, lane, jnp.where(lane == HALF, HALF, lane - HALF))
    kx = k_slot.astype(F32) * WAVE
    kx2 = kx * kx
    edge_k = (lane == 0) | (lane == HALF)
    weight_k = jnp.where(edge_k, 1.0, 2.0)
    block = 256
    turn_cos = phase_ref[0:1, :]
    turn_sin = phase_ref[1:2, :]

    def channel_block(i, corner):
        at = pl.multiple_of(i * block, block)
        v_hi = v_hi_ref[pl.ds(at, block), :]
        v_lo = v_lo_ref[pl.ds(at, block), :]
        dh = dens_hi_ref[...]
        first = dot_nt(v_hi, dh) + dot_nt(v_lo, dh) + dot_nt(v_hi, dens_lo_ref[...])
        f_hi, f_lo = split(first)
        spec = (
            dot_nt(f_hi, v_hi_ref[...]) + dot_nt(f_lo, v_hi_ref[...]) + dot_nt(f_hi, v_lo_ref[...])
        )
        chan = at + lax.broadcasted_iota(jnp.int32, (block, 1), 0)
        l_slot = jnp.where(chan < HALF, chan, jnp.where(chan == HALF, HALF, chan - HALF))
        ky = l_slot.astype(F32) * WAVE
        weight_l = jnp.where((chan == 0) | (chan == HALF), 1.0, 2.0)
        scale = (weight_l * (-2.0 / (NP * NP))) * weight_k
        pot = spec * (scale / (kx2 + ky * ky + MU2))
        corner = jnp.where(i == HALF // block, pot[0:1, HALF : HALF + 1], corner)
        pot_c = pot[:, 0:HALF]
        pot_s = pot[:, HALF:NP]
        turned = jnp.concatenate(
            [pot_c * turn_cos + pot_s * turn_sin, pot_s * turn_cos - pot_c * turn_sin], axis=1
        )
        p_hi, p_lo = split(turned)
        uh = u_hi_ref[...]
        ba_ref[:, pl.ds(at, block)] = (
            dot_nt(uh, p_hi) + dot_nt(u_lo_ref[...], p_hi) + dot_nt(uh, p_lo)
        )
        return corner

    corner = lax.fori_loop(0, NP // block, channel_block, jnp.zeros((1, 1), F32))

    row_at = lax.broadcasted_iota(jnp.int32, (win, 1), 0)
    grid_row = (tile - 1) * tile_rows + row_at
    inside = ((grid_row >= 0) & (grid_row < NG)).astype(F32)
    b_all = ba_ref[0:win, :] * inside
    a_all = ba_ref[win : 2 * win, :] * inside
    ky2 = kx2
    sign = (1 - 2 * (row_at % 2)).astype(F32)
    corner_col = inside * sign * corner * (-math.pi * math.pi)
    lane_half = lax.broadcasted_iota(jnp.int32, (1, HALF), 1)

    def store(field, value):
        hi, lo = split(value)
        l_hi_ref[field] = hi
        l_lo_ref[field] = lo

    store(0, a_all)
    store(
        1,
        jnp.concatenate([half_lane * b_all[:, HALF:NP], -half_lane * b_all[:, 0:HALF]], axis=1),
    )
    store(2, (MU2 + ky2) * b_all)
    store(
        3,
        jnp.concatenate(
            [
                half_lane * a_all[:, HALF:NP],
                jnp.where(lane_half == 0, corner_col, -half_lane * a_all[:, 0:HALF]),
            ],
            axis=1,
        ),
    )
    store(4, -ky2 * b_all)

    def one_field(f, carry):
        lh = l_hi_ref[f]
        vh = v_hi_ref[...]
        out = dot_nn(lh, vh) + dot_nn(l_lo_ref[f], vh) + dot_nn(lh, v_lo_ref[...])
        row = pl.multiple_of(tile * tile_rows, 8)
        out = out + jnp.where(f == 2, 2.0, 0.0) * dens_ref[pl.ds(row, win), :]
        lens_ref[0, f] = out[tile_rows : 2 * tile_rows, :]
        hi, lo = split(out)
        tab_hi_ref[f] = hi
        tab_lo_ref[f] = lo
        return carry

    lax.fori_loop(0, 5, one_field, 0)


def ray_kernel(info_ref, inbox_ref, cell_ref, offset_ref, tab_hi_ref, tab_lo_ref, out_ref, *, tile_rows):
    batch = info_ref[0]
    first_plane = info_ref[1]
    tile = info_ref[2]
    active = info_ref[3]
    rays = out_ref.shape[1]
    fields, win, _ = tab_hi_ref.shape
    span = float(tile_rows - 1)
    n = RAY_CHUNK
    col_iota = (lax.broadcasted_iota(jnp.int32, (NG, n), 0) - NG // 2).astype(F32).astype(BF16)
    row_iota = lax.broadcasted_iota(jnp.int32, (win, n), 0)
    unit_row = lax.broadcasted_iota(jnp.int32, (6, n), 0)
    unit = jnp.where((unit_row == 2) | (unit_row == 5), 1.0, 0.0)
    zero = jnp.zeros((), BF16)

    def chunk(i, carry):
        at = pl.multiple_of(i * n, n)
        state = jnp.where(first_plane > 0, unit, inbox_ref[:, pl.ds(at, n)])
        cell = cell_ref[pl.ds(batch, 1), pl.ds(at, n)]
        base_row = (tile * tile_rows + cell // NG).astype(F32) + offset_ref[0, pl.ds(batch, 1), pl.ds(at, n)]
        base_col = (cell % NG).astype(F32) + offset_ref[1, pl.ds(batch, 1), pl.ds(at, n)]
        dx = state[0:1]
        dy = state[1:2]
        row_pos = base_row + span * jnp.tanh(dx / span)
        col_pos = base_col + span * jnp.tanh(dy / span)
        row_floor = jnp.floor(row_pos)
        col_floor = jnp.floor(col_pos)
        frac_row = row_pos - row_floor
        frac_col = col_pos - col_floor
        row_id = row_floor.astype(jnp.int32) - (tile - 1) * tile_rows
        row_w = jnp.where(row_iota == row_id, 1.0 - frac_row, 0.0) + jnp.where(
            row_iota == row_id + 1, frac_row, 0.0
        )
        far = 4.0 * NG
        c0 = jnp.where((col_floor >= 0.0) & (col_floor < NG), col_floor - NG // 2, far).astype(BF16)
        c1 = jnp.where(
            (col_floor >= -1.0) & (col_floor < NG - 1.0), col_floor + (1.0 - NG // 2), far
        ).astype(BF16)
        g0_hi, g0_lo = split(1.0 - frac_col)
        g1_hi, g1_lo = split(frac_col)
        here = col_iota == c0
        there = col_iota == c1
        w_hi = jnp.where(here, g0_hi, jnp.where(there, g1_hi, zero))
        w_lo = jnp.where(here, g0_lo, jnp.where(there, g1_lo, zero))
        values = []
        for f in range(fields):
            th = tab_hi_ref[f]
            along = dot_nn(th, w_hi) + dot_nn(tab_lo_ref[f], w_hi) + dot_nn(th, w_lo)
            values.append(jnp.sum(along * row_w, axis=0, keepdims=True))
        ax, ay, hxx, hxy, hyy = values
        a11 = state[2:3]
        a12 = state[3:4]
        a21 = state[4:5]
        a22 = state[5:6]
        out_ref[:, pl.ds(at, n)] = jnp.concatenate(
            [
                dx - LENS_WEIGHT * ax,
                dy - LENS_WEIGHT * ay,
                a11 - LENS_WEIGHT * (hxx * a11 + hxy * a21),
                a12 - LENS_WEIGHT * (hxx * a12 + hxy * a22),
                a21 - LENS_WEIGHT * (hxy * a11 + hyy * a21),
                a22 - LENS_WEIGHT * (hxy * a12 + hyy * a22),
            ],
            axis=0,
        )
        return carry

    @pl.when(active > 0)
    def _():
        lax.fori_loop(0, rays // n, chunk, 0)

    @pl.when(active == 0)
    def _():
        out_ref[...] = jnp.zeros(out_ref.shape, F32)


def trig_table(rows):
    m = np.arange(rows)[:, None]
    k = np.arange(HALF)[None, :]
    phase = (m * k % NP) * (2.0 * np.pi / NP)
    table = np.concatenate([np.cos(phase), np.sin(phase)], axis=1)
    table[:, HALF] = 1.0 - 2.0 * (np.arange(rows) % 2)
    return table


def per_device(block_dest, particle_cell, particle_offset, particle_mass, ray_cell, ray_offset):
    tiles = lax.axis_size("tile")
    planes = lax.axis_size("plane")
    tile_rows = NG // tiles
    tile_now = lax.axis_index("tile")
    plane_now = lax.axis_index("plane")
    blocks = particle_cell.shape[1]
    block_len = particle_cell.shape[2]
    cap = 2 * blocks // tiles
    win = 3 * tile_rows

    outgoing = pl.pallas_call(
        route_kernel,
        out_shape=jax.ShapeDtypeStruct((tiles * 4 * cap, block_len), F32),
        in_specs=[smem_spec(), vmem_spec(), vmem_spec(), vmem_spec()],
        out_specs=vmem_spec(),
        scratch_shapes=[pltpu.SMEM((tiles,), jnp.int32)],
        name="route",
    )(block_dest.reshape(-1), particle_cell, particle_offset, particle_mass)
    incoming = lax.all_to_all(
        outgoing.reshape(tiles, 4 * cap, block_len), "tile", split_axis=0, concat_axis=0, tiled=True
    )

    scaling = math.sqrt(tile_rows * NG / (BLOCKS_DEV * block_len))
    rows_acc = -(-(tile_rows + 1) // 16) * 16
    canvas_rows = tile_rows + 8
    canvas = pl.pallas_call(
        lambda a, b, c: deposit_kernel(a, b, c, scaling=scaling, tile_rows=tile_rows),
        out_shape=jax.ShapeDtypeStruct((canvas_rows, NG), F32),
        in_specs=[vmem_spec()],
        out_specs=vmem_spec(),
        scratch_shapes=[VMEM((4 * rows_acc, NG), F32)],
        name="deposit",
    )(incoming)

    groups = [[i for i in range(tiles) if i % 2 == p] for p in (0, 1)]
    mine = lax.all_gather(canvas, "tile", axis=0, tiled=False, axis_index_groups=groups)
    other = lax.ppermute(mine, "tile", [(i, i ^ 1) for i in range(tiles)])

    v = trig_table(NG).T.astype(np.float32)
    v_hi = v.astype(jnp.bfloat16)
    v_lo = (v - v_hi.astype(np.float32)).astype(jnp.bfloat16)
    w0 = trig_table(win).astype(np.float32)
    k_index = lax.broadcasted_iota(jnp.int32, (1, HALF), 1)
    origin = (tile_now - 1) * tile_rows + NP
    turn = (k_index * origin % NP).astype(F32) * WAVE
    phase = jnp.concatenate([jnp.cos(turn), jnp.sin(turn)], axis=0)
    info = jnp.stack([tile_now, tile_now % 2]).astype(jnp.int32)
    lens, tab_hi, tab_lo = pl.pallas_call(
        lambda *refs: fields_kernel(*refs, tile_rows=tile_rows),
        out_shape=(
            jax.ShapeDtypeStruct((1, 5, tile_rows, NG), F32),
            jax.ShapeDtypeStruct((5, win, NG), BF16),
            jax.ShapeDtypeStruct((5, win, NG), BF16),
        ),
        in_specs=[smem_spec()] + [vmem_spec()] * 6,
        out_specs=(vmem_spec(), vmem_spec(), vmem_spec()),
        scratch_shapes=[
            VMEM((NG + 2 * tile_rows, NG), F32),
            VMEM((NG, NG), BF16),
            VMEM((NG, NG), BF16),
            VMEM((2 * win, NP), BF16),
            VMEM((2 * win, NP), BF16),
            VMEM((2 * win, NP), F32),
            VMEM((5, win, NP), BF16),
            VMEM((5, win, NP), BF16),
        ],
        name="fields",
    )(info, mine, other, jnp.asarray(v_hi), jnp.asarray(v_lo), jnp.asarray(w0), phase)

    batches = ray_cell.shape[0]
    rays = ray_cell.shape[1]
    ring = [(i, (i + 1) % planes) for i in range(planes)]
    inbox = jnp.zeros((6, rays), F32)
    states = []
    for turn_index in range(batches + planes - 1):
        batch = turn_index - plane_now
        active = (batch >= 0) & (batch < batches)
        ray_info = jnp.stack(
            [
                jnp.clip(batch, 0, batches - 1),
                (plane_now == 0).astype(jnp.int32),
                tile_now,
                active.astype(jnp.int32),
            ]
        ).astype(jnp.int32)
        moved = pl.pallas_call(
            lambda *refs: ray_kernel(*refs, tile_rows=tile_rows),
            out_shape=jax.ShapeDtypeStruct((6, rays), F32),
            in_specs=[smem_spec()] + [vmem_spec()] * 5,
            out_specs=vmem_spec(),
            name="rays",
        )(ray_info, inbox, ray_cell, ray_offset, tab_hi, tab_lo)
        states.append(moved)
        if turn_index < batches + planes - 2:
            inbox = lax.ppermute(moved, "plane", ring)
    ray_maps = lax.dynamic_slice_in_dim(jnp.stack(states), plane_now, batches, axis=0)
    return (lens, ray_maps[None])


def solution(mesh):
    return jax.shard_map(
        per_device,
        mesh=mesh,
        in_specs=(
            P("plane", "tile", None),
            P("plane", "tile", None),
            P("plane", None, "tile", None),
            P("plane", "tile", None),
            P(None, "tile"),
            P(None, None, "tile"),
        ),
        out_specs=(P("plane", None, "tile", None), P("plane", None, None, "tile")),
        check_vma=False,
    )
```

time: 437 us -> 162 us (0.37); the launches traced: 429 us -> 161 us
  matrix products: 269 us -> 0 us
  Pallas kernels: 0 us -> 69.2 us
  waiting for transfers between devices: 53.6 us -> 15.7 us
  blocking collectives: 35.7 us -> 10.2 us
  starting transfers between devices: 25.5 us -> 40.4 us
  other arithmetic: 18.1 us -> 4.97 us
    dot_general x36 -> x0, matrix products: 269 us -> none  [the longest x7 95 us: interpolate(): jnp.einsum('frc,cq->frq', window, col_weights, precision=HIGHEST_PRECISIO...]
    pallas_call x0 -> x9, Pallas kernels: none -> 69.2 us  [the longest x6 37.1 us: per_device(): pl.pallas_call(lambda *refs: ray_kernel(*refs, tile_rows=tile_rows), out_...]
    all_to_all x1 -> x0, blocking collectives: 35.7 us -> none  [per_device(): lax.all_to_all(jnp.stack([rows_re, rows_im], axis=1), 'tile', split_axis=...]
    ppermute x10 -> x7, waiting for transfers between devices: 40.1 us -> 12.6 us  [the longest x6 12.6 us: per_device(): inbox = lax.ppermute(moved, 'plane', ring)]
    ppermute x10 -> x7, starting transfers between devices: 16.5 us -> 36.2 us  [the longest x6 36.1 us: per_device(): inbox = lax.ppermute(moved, 'plane', ring)]
    all_to_all x2 -> x1, waiting for transfers between devices: 13.6 us -> 3.15 us  [per_device(): lax.all_to_all(outgoing.reshape(tiles, 4 * cap, block_len), 'tile', split...]
    all_gather x0 -> x1, blocking collectives: none -> 10.2 us  [per_device(): lax.all_gather(canvas, 'tile', axis=0, tiled=False, axis_index_groups=gro...]
    pallas_call x0 -> x1, local copies, waits for them, and re-layouts: none -> 8.48 us  [per_device(): pl.pallas_call(lambda *refs: ray_kernel(*refs, tile_rows=tile_rows), out_...]
  transfers between devices with their start and end apart: 12 -> 8, of which waited for: 12 -> 7; matrix products, arithmetic and copies ran while one was open for 2% -> 6% of each run, Pallas kernels for 0% -> 0%
where the time goes in v1:
time: 162 us; the launch traced here: 161 us
  Pallas kernels  69.2 us (43%)
  starting transfers between devices  40.4 us (25%)
  local copies, waits for them, and re-layouts  19.9 us (12%)
  waiting for transfers between devices  15.7 us (10%)
  blocking collectives  10.2 us (6%)
  other arithmetic  4.97 us (3%)
    pallas_call x6, Pallas kernels, per_device(): pl.pallas_call(lambda *refs: ray_kernel(*refs, tile_rows=tile_rows), out_...  37.1 us
    ppermute x6, starting transfers between devices, per_device(): inbox = lax.ppermute(moved, 'plane', ring)  36.1 us
    pallas_call x1, Pallas kernels, per_device(): pl.pallas_call(lambda *refs: fields_kernel(*refs, tile_rows=tile_rows), o...  19.2 us
    ppermute x6, waiting for transfers between devices, per_device(): inbox = lax.ppermute(moved, 'plane', ring)  12.6 us
    pallas_call x1, Pallas kernels, per_device(): pl.pallas_call(lambda a, b, c: deposit_kernel(a, b, c, scaling=scaling, t...  10.8 us
    all_gather x1, blocking collectives, per_device(): lax.all_gather(canvas, 'tile', axis=0, tiled=False, axis_index_groups=gro...  10.2 us
    unnamed x30, local copies, waits for them, and re-layouts  10 us
    pallas_call x1, local copies, waits for them, and re-layouts, per_device(): pl.pallas_call(lambda *refs: ray_kernel(*refs, tile_rows=tile_rows), out_...  8.48 us
  transfers between devices with their start and end apart: 8, of which 7 were waited for; matrix products, arithmetic and copies ran while one was open for 6% of the time, Pallas kernels for 0%

profile of v1, /device:TPU:26, one launch (start us, length us, event | category | flops | bytes accessed | tf_op | source)
XLA Modules:
  0.0 161.2 jit_solution(7201054535301368990)
XLA Ops:
  0.6 2.1 %route.1 = f32[512,128]{1,0:T(8,128)} custom-call(s32[64]{0:T(128)} %bitcast.41, s32[1,64,128]{2,1,0:T(8,128)} %cell_ref.1, f32[1,2,64,128]{3,2,1,0:T(8,128)} %offset_ref.1, f32[1,64,128]{2,1,0:T(8,128)} %mass_ref.1), custom_call_target="tpu_custom_call" | custom-call | tf_op jit(solution)/shard_map/route/pallas_call | solution.py:368
  2.8 4.3 %all-to-all-start = ((f32[8,64,128]{2,1,0:T(8,128)}), f32[8,64,128]{2,1,0:T(8,128)S(1)}, u32[]{:S(2)}, u32[]{:S(2)}) async-start(f32[8,64,128]{2,1,0:T(8,128)} %bitcast.39), calls=%async_computation | async-start | bytes 524288 | tf_op jit(solution)/shard_map/all_to_all | solution.py:376
  7.0 0.6 pad_add_fusion.refs_0_
  7.6 0.6 pad_add_fusion.1.refs_0_
  8.2 0.6 pad_add_fusion.2.refs_0_
  8.8 0.6 pad_add_fusion.3.refs_0_
  9.3 3.1 %all-to-all-done.a = f32[8,64,128]{2,1,0:T(8,128)S(1)} async-done(((f32[8,64,128]{2,1,0:T(8,128)}), f32[8,64,128]{2,1,0:T(8,128)S(1)}, u32[]{:S(2)}, u32[]{:S(2)}) %all-to-all-start) | async-done | bytes 262176 | tf_op jit(solution)/shard_map/all_to_all | solution.py:376
  12.5 0.7 copy-done.5
  13.2 10.8 %deposit.1 = f32[72,512]{1,0:T(8,128)} custom-call(f32[8,64,128]{2,1,0:T(8,128)} %copy-done.5), custom_call_target="tpu_custom_call" | custom-call | tf_op jit(solution)/shard_map/deposit/pallas_call | solution.py:383
  24.0 10.2 %all-gather = f32[288,512]{1,0:T(8,128)S(1)} all-gather(f32[72,512]{1,0:T(8,128)} %deposit.1), channel_id=2, replica_groups={{0,2,4,6},{1,3,5,7},{8,10,12,14},{9,11,13,15},{16,18,20,22},{17,19,21,2..., dimensions={0}, use_global_device_ids=true | all-gather | bytes 737280 | tf_op jit(solution)/shard_map/all_gather | solution.py:393
  34.3 0.7 pad_add_fusion.4.refs_0_
  34.9 0.6 pad_add_fusion.5.refs_0_
  35.6 0.6 pad_add_fusion.6.refs_0_
  36.2 0.1 pad_add_fusion.7
  36.3 0.1 fusion.3
  36.3 0.6 pad_maximum_fusion.refs_6_
  37.0 0.8 copy-done.6
  37.8 19.2 %fields.1 = (f32[1,5,64,512]{3,2,1,0:T(8,128)}, bf16[5,192,512]{2,1,0:T(8,128)(2,1)}, bf16[5,192,512]{2,1,0:T(8,128)(2,1)}) custom-call(s32[2]{0:T(128)} %pad_add_fusion.refs_0_, f32[4,72,512]{2,1,0:T(8,128)} %bitcast.38, f32[4,72,512]{2,1,0:T(8,128)} %copy-done.6, bf16[1024,512]{1,0:T(8,128)(2,1)} %constant.61.clone.refs_3_, ...), custom_call_target="tpu_custom_call" | custom-call | tf_op jit(solution)/shard_map/fields/pallas_call | solution.py:405
  57.0 0.6 broadcast_in_dim.6.refs_1_
  57.7 2.2 %rays.7 = f32[6,2048]{1,0:T(8,128)} custom-call(s32[4]{0:T(128)} %pad_add_fusion.1.refs_0_, f32[6,2048]{1,0:T(8,128)} %broadcast_in_dim.6.refs_1_, s32[4,2048]{1,0:T(4,128)} %refs_2_.12, f32[2,4,2048]{2,1,0:T(4,128)} %refs_3_.13, bf16[5,192,512]{2,1,0:T(8,128)(2,1)} %get-tuple-element.6.refs_4_, bf16[5,192,512]{2,1,0:T(8,128)(2,1)} %get-tuple-element.7.refs_5_), custom_call_target="tpu_custom_call" | custom-call | tf_op jit(solution)/shard_map/rays/pallas_call | solution.py:443
  59.9 8.1 %collective-permute-start.1 = (f32[6,2048]{1,0:T(8,128)}, f32[6,2048]{1,0:T(8,128)S(1)}, u32[]{:S(2)}, u32[]{:S(2)}) collective-permute-start(f32[6,2048]{1,0:T(8,128)} %rays.7), channel_id=1, source_target_pairs={{0,8},{8,16},{16,24},{24,0},{1,9},{9,17},{17,25},{25,1},{2,10},{10... | collective-permute-start | bytes 147464 | tf_op jit(solution)/shard_map/ppermute | solution.py:452
  68.0 0.9 bitcast_dynamic-update-slice_fusion.6
  68.9 1.4 collective-permute-done.1.refs_1_
  70.3 0.6 copy-done.11
  70.9 2.2 %rays.8 = f32[6,2048]{1,0:T(8,128)} custom-call(s32[4]{0:T(128)} %pad_add_fusion.2.refs_0_, f32[6,2048]{1,0:T(8,128)} %copy-done.11, s32[4,2048]{1,0:T(4,128)} %refs_2_.12, f32[2,4,2048]{2,1,0:T(4,128)} %refs_3_.13, bf16[5,192,512]{2,1,0:T(8,128)(2,1)} %get-tuple-element.6.refs_4_, bf16[5,192,512]{2,1,0:T(8,128)(2,1)} %get-tuple-element.7.refs_5_), custom_call_target="tpu_custom_call" | custom-call | tf_op jit(solution)/shard_map/rays/pallas_call | solution.py:443
  73.1 12.1 %collective-permute-start.2 = (f32[6,2048]{1,0:T(8,128)}, f32[6,2048]{1,0:T(8,128)S(1)}, u32[]{:S(2)}, u32[]{:S(2)}) collective-permute-start(f32[6,2048]{1,0:T(8,128)} %rays.8), channel_id=1, source_target_pairs={{0,8},{8,16},{16,24},{24,0},{1,9},{9,17},{17,25},{25,1},{2,10},{10... | collective-permute-start | bytes 147464 | tf_op jit(solution)/shard_map/ppermute | solution.py:452
  85.2 0.9 bitcast_dynamic-update-slice_fusion.5
  86.1 1.3 collective-permute-done.2.refs_1_
  87.4 0.6 copy-done.7
  88.0 2.2 %rays.9 = f32[6,2048]{1,0:T(8,128)} custom-call(s32[4]{0:T(128)} %pad_add_fusion.3.refs_0_, f32[6,2048]{1,0:T(8,128)} %copy-done.7, s32[4,2048]{1,0:T(4,128)} %refs_2_.12, f32[2,4,2048]{2,1,0:T(4,128)} %refs_3_.13, bf16[5,192,512]{2,1,0:T(8,128)(2,1)} %get-tuple-element.6.refs_4_, bf16[5,192,512]{2,1,0:T(8,128)(2,1)} %get-tuple-element.7.refs_5_), custom_call_target="tpu_custom_call" | custom-call | tf_op jit(solution)/shard_map/rays/pallas_call | solution.py:443
  90.3 11.9 %collective-permute-start.3 = (f32[6,2048]{1,0:T(8,128)}, f32[6,2048]{1,0:T(8,128)S(1)}, u32[]{:S(2)}, u32[]{:S(2)}) collective-permute-start(f32[6,2048]{1,0:T(8,128)} %rays.9), channel_id=1, source_target_pairs={{0,8},{8,16},{16,24},{24,0},{1,9},{9,17},{17,25},{25,1},{2,10},{10... | collective-permute-start | bytes 147464 | tf_op jit(solution)/shard_map/ppermute | solution.py:452
  102.2 0.9 bitcast_dynamic-update-slice_fusion.4
  103.1 1.3 collective-permute-done.3.refs_1_
  104.4 0.6 copy-done.8
  105.1 10.1 %rays.10 = f32[6,2048]{1,0:T(8,128)} custom-call(s32[4]{0:T(128)} %pad_add_fusion.4.refs_0_, f32[6,2048]{1,0:T(8,128)} %copy-done.8, s32[4,2048]{1,0:T(4,128)} %refs_2_.12, f32[2,4,2048]{2,1,0:T(4,128)} %refs_3_.13, bf16[5,192,512]{2,1,0:T(8,128)(2,1)} %get-tuple-element.6.refs_4_, bf16[5,192,512]{2,1,0:T(8,128)(2,1)} %get-tuple-element.7.refs_5_), custom_call_target="tpu_custom_call" | custom-call | tf_op jit(solution)/shard_map/rays/pallas_call | solution.py:443
  115.2 4.1 %collective-permute-start.4 = (f32[6,2048]{1,0:T(8,128)}, f32[6,2048]{1,0:T(8,128)S(1)}, u32[]{:S(2)}, u32[]{:S(2)}) collective-permute-start(f32[6,2048]{1,0:T(8,128)} %rays.10), channel_id=1, source_target_pairs={{0,8},{8,16},{16,24},{24,0},{1,9},{9,17},{17,25},{25,1},{2,10},{10... | collective-permute-start | bytes 147464 | tf_op jit(solution)/shard_map/ppermute | solution.py:452
  119.2 0.9 bitcast_dynamic-update-slice_fusion.3
  120.1 1.3 collective-permute-done.4.refs_1_
  121.4 0.6 copy-done.9
  122.1 10.1 %rays.11 = f32[6,2048]{1,0:T(8,128)} custom-call(s32[4]{0:T(128)} %pad_add_fusion.5.refs_0_, f32[6,2048]{1,0:T(8,128)} %copy-done.9, s32[4,2048]{1,0:T(4,128)} %refs_2_.12, f32[2,4,2048]{2,1,0:T(4,128)} %refs_3_.13, bf16[5,192,512]{2,1,0:T(8,128)(2,1)} %get-tuple-element.6.refs_4_, bf16[5,192,512]{2,1,0:T(8,128)(2,1)} %get-tuple-element.7.refs_5_), custom_call_target="tpu_custom_call" | custom-call | tf_op jit(solution)/shard_map/rays/pallas_call | solution.py:443
  132.2 0.9 bitcast_dynamic-update-slice_fusion.2
  133.1 3.6 %collective-permute-done.5.refs_1_ = f32[6,2048]{1,0:T(8,128)S(1)} collective-permute-done((f32[6,2048]{1,0:T(8,128)}, f32[6,2048]{1,0:T(8,128)S(1)}, u32[]{:S(2)}, u32[]{:S(2)}) %collective-permute-start.5) | collective-permute-done | bytes 49184 | tf_op jit(solution)/shard_map/ppermute | solution.py:452
  136.7 0.6 copy-done.10
  137.3 10.1 %rays.12 = f32[6,2048]{1,0:T(8,128)} custom-call(s32[4]{0:T(128)} %pad_add_fusion.6.refs_0_, f32[6,2048]{1,0:T(8,128)} %copy-done.10, s32[4,2048]{1,0:T(4,128)} %refs_2_.12, f32[2,4,2048]{2,1,0:T(4,128)} %refs_3_.13, bf16[5,192,512]{2,1,0:T(8,128)(2,1)} %get-tuple-element.6.refs_4_, bf16[5,192,512]{2,1,0:T(8,128)(2,1)} %get-tuple-element.7.refs_5_), custom_call_target="tpu_custom_call" | custom-call | tf_op jit(solution)/shard_map/rays/pallas_call | solution.py:443
  147.4 0.9 bitcast_dynamic-update-slice_fusion.1
  148.3 3.6 %collective-permute-done.6 = f32[6,2048]{1,0:T(8,128)S(1)} collective-permute-done((f32[6,2048]{1,0:T(8,128)}, f32[6,2048]{1,0:T(8,128)S(1)}, u32[]{:S(2)}, u32[]{:S(2)}) %collective-permute-start.6) | collective-permute-done | bytes 49184 | tf_op jit(solution)/shard_map/ppermute | solution.py:452
  151.9 8.5 %rays.13 = f32[7,6,2048]{2,1,0:T(8,128)S(1)} fusion(f32[7,6,2048]{2,1,0:T(8,128)S(1)} %bitcast_dynamic-update-slice_fusion.1, s32[4]{0:T(128)S(1)} %pad_add_fusion.7, f32[6,2048]{1,0:T(8,128)S(1)} %collective-permute-done.6, s32[4,2048]{1,0:T(4,128)S(1)} %copy-done.4, f32[2,4,2048]{2,1,0:T(4,128)S(1)} %copy-done.2, bf16[5,192,512]{2,1,0:T(8,128)(2,1)S(1)} %copy-done, ...), kind=kCustom, calls=%fused_computation.1 | custom fusion | bytes 2195968 | tf_op jit(solution)/shard_map/rays/pallas_call | solution.py:443
  160.4 0.8 copy.13
  (22 shorter events, 0.1 us)
Async XLA Ops:
  2.8 9.7 %all-to-all-start = ((f32[8,64,128]{2,1,0:T(8,128)}), f32[8,64,128]{2,1,0:T(8,128)S(1)}, u32[]{:S(2)}, u32[]{:S(2)}) async-start(f32[8,64,128]{2,1,0:T(8,128)} %bitcast.39), calls=%async_computation | async-start | bytes 524288 | tf_op jit(solution)/shard_map/all_to_all | solution.py:376
  12.5 0.7 copy-start.5
  34.2 2.8 %copy-start.3 = (f32[288,512]{1,0:T(8,128)}, f32[288,512]{1,0:T(8,128)S(1)}, u32[]{:S(2)}) copy-start(f32[288,512]{1,0:T(8,128)S(1)} %all-gather) | copy-start | bytes 1769476
  34.2 2.8 %collective-permute-start = (f32[4,72,512]{2,1,0:T(8,128)S(1)}, f32[4,72,512]{2,1,0:T(8,128)S(1)}, u32[]{:S(2)}, u32[]{:S(2)}) collective-permute-start(f32[4,72,512]{2,1,0:T(8,128)S(1)} %bitcast.37), channel_id=1, source_target_pairs={{0,1},{1,0},{2,3},{3,2},{4,5},{5,4},{6,7},{7,6},{8,9},{9,8},{10,11... | collective-permute-start | bytes 1769480 | tf_op jit(solution)/shard_map/ppermute | solution.py:394
  37.0 0.8 copy-start.6
  59.9 10.4 %collective-permute-start.1 = (f32[6,2048]{1,0:T(8,128)}, f32[6,2048]{1,0:T(8,128)S(1)}, u32[]{:S(2)}, u32[]{:S(2)}) collective-permute-start(f32[6,2048]{1,0:T(8,128)} %rays.7), channel_id=1, source_target_pairs={{0,8},{8,16},{16,24},{24,0},{1,9},{9,17},{17,25},{25,1},{2,10},{10... | collective-permute-start | bytes 147464 | tf_op jit(solution)/shard_map/ppermute | solution.py:452
  70.3 0.6 copy-start.11
  73.1 14.3 %collective-permute-start.2 = (f32[6,2048]{1,0:T(8,128)}, f32[6,2048]{1,0:T(8,128)S(1)}, u32[]{:S(2)}, u32[]{:S(2)}) collective-permute-start(f32[6,2048]{1,0:T(8,128)} %rays.8), channel_id=1, source_target_pairs={{0,8},{8,16},{16,24},{24,0},{1,9},{9,17},{17,25},{25,1},{2,10},{10... | collective-permute-start | bytes 147464 | tf_op jit(solution)/shard_map/ppermute | solution.py:452
  87.4 0.6 copy-start.7
  90.3 14.1 %collective-permute-start.3 = (f32[6,2048]{1,0:T(8,128)}, f32[6,2048]{1,0:T(8,128)S(1)}, u32[]{:S(2)}, u32[]{:S(2)}) collective-permute-start(f32[6,2048]{1,0:T(8,128)} %rays.9), channel_id=1, source_target_pairs={{0,8},{8,16},{16,24},{24,0},{1,9},{9,17},{17,25},{25,1},{2,10},{10... | collective-permute-start | bytes 147464 | tf_op jit(solution)/shard_map/ppermute | solution.py:452
  104.4 0.6 copy-start.8
  115.2 6.3 %collective-permute-start.4 = (f32[6,2048]{1,0:T(8,128)}, f32[6,2048]{1,0:T(8,128)S(1)}, u32[]{:S(2)}, u32[]{:S(2)}) collective-permute-start(f32[6,2048]{1,0:T(8,128)} %rays.10), channel_id=1, source_target_pairs={{0,8},{8,16},{16,24},{24,0},{1,9},{9,17},{17,25},{25,1},{2,10},{10... | collective-permute-start | bytes 147464 | tf_op jit(solution)/shard_map/ppermute | solution.py:452
  121.4 0.6 copy-start.9
  132.2 4.5 %collective-permute-start.5 = (f32[6,2048]{1,0:T(8,128)}, f32[6,2048]{1,0:T(8,128)S(1)}, u32[]{:S(2)}, u32[]{:S(2)}) collective-permute-start(f32[6,2048]{1,0:T(8,128)} %rays.11), channel_id=1, source_target_pairs={{0,8},{8,16},{16,24},{24,0},{1,9},{9,17},{17,25},{25,1},{2,10},{10... | collective-permute-start | bytes 147464 | tf_op jit(solution)/shard_map/ppermute | solution.py:452
  133.1 18.8 %copy-start = (bf16[5,192,512]{2,1,0:T(8,128)(2,1)S(1)}, bf16[5,192,512]{2,1,0:T(8,128)(2,1)}, u32[]{:S(2)}) copy-start(bf16[5,192,512]{2,1,0:T(8,128)(2,1)} %get-tuple-element.6.refs_4_) | copy-start | bytes 2949124
  133.1 18.8 %copy-start.1 = (bf16[5,192,512]{2,1,0:T(8,128)(2,1)S(1)}, bf16[5,192,512]{2,1,0:T(8,128)(2,1)}, u32[]{:S(2)}) copy-start(bf16[5,192,512]{2,1,0:T(8,128)(2,1)} %get-tuple-element.7.refs_5_) | copy-start | bytes 2949124
  136.7 0.6 copy-start.10
  147.4 4.5 %copy-start.2 = (f32[2,4,2048]{2,1,0:T(4,128)S(1)}, f32[2,4,2048]{2,1,0:T(4,128)}, u32[]{:S(2)}) copy-start(f32[2,4,2048]{2,1,0:T(4,128)} %refs_3_.13) | copy-start | bytes 196612
  147.4 4.5 %copy-start.4 = (s32[4,2048]{1,0:T(4,128)S(1)}, s32[4,2048]{1,0:T(4,128)}, u32[]{:S(2)}) copy-start(s32[4,2048]{1,0:T(4,128)} %refs_2_.12) | copy-start | bytes 98308
  147.4 4.5 %collective-permute-start.6 = (f32[6,2048]{1,0:T(8,128)}, f32[6,2048]{1,0:T(8,128)S(1)}, u32[]{:S(2)}, u32[]{:S(2)}) collective-permute-start(f32[6,2048]{1,0:T(8,128)} %rays.12), channel_id=1, source_target_pairs={{0,8},{8,16},{16,24},{24,0},{1,9},{9,17},{17,25},{25,1},{2,10},{10... | collective-permute-start | bytes 147464 | tf_op jit(solution)/shard_map/ppermute | solution.py:452

commit v2 on v1

v2 whole, which is shorter than its diff:
```python
import math

import jax
import jax.numpy as jnp
from jax import lax
from jax.experimental import pallas as pl
from jax.experimental.pallas import tpu as pltpu
from jax.sharding import PartitionSpec as P

NG = 512
NP = 2 * NG
HALF = NP // 2
BLOCKS_DEV = 64

LENS_WEIGHT = 0.15
SCREEN_SCALE = 0.5
MU2 = (SCREEN_SCALE * 2.0 * math.pi / NP) ** 2
WAVE = 2.0 * math.pi / NP
F32 = jnp.float32
BF16 = jnp.bfloat16
VMEM = pltpu.VMEM
RAY_CHUNK = 512
GROUP = 2
SUB = 16
TIERS = (5, 6, 7)


def vmem_spec():
    return pl.BlockSpec(memory_space=pltpu.VMEM)


def hbm_spec():
    return pl.BlockSpec(memory_space=pltpu.HBM)


def params(mib):
    return pltpu.CompilerParams(vmem_limit_bytes=mib * 1024 * 1024)


def smem_spec():
    return pl.BlockSpec(memory_space=pltpu.SMEM)


def split(x):
    hi = x.astype(BF16)
    return hi, (x - hi.astype(F32)).astype(BF16)


def dot_nt(a, b):
    return lax.dot_general(a, b, (((1,), (1,)), ((), ())), preferred_element_type=F32)


def dot_nn(a, b):
    return lax.dot_general(a, b, (((1,), (0,)), ((), ())), preferred_element_type=F32)


def route_kernel(dest_hbm, cell_hbm, offset_hbm, mass_hbm, out_ref, dest_ref, cell_ref, offset_ref, mass_ref, count_ref, sems):
    copies = [
        pltpu.make_async_copy(src, dst, sems.at[i])
        for i, (src, dst) in enumerate(
            (
                (dest_hbm, dest_ref),
                (cell_hbm, cell_ref),
                (offset_hbm, offset_ref),
                (mass_hbm, mass_ref),
            )
        )
    ]
    for copy in copies:
        copy.start()
    tiles = count_ref.shape[0]
    blocks = cell_ref.shape[1]
    cap = out_ref.shape[0] // (4 * tiles)
    out_ref[...] = jnp.zeros(out_ref.shape, F32)
    for t in range(tiles):
        count_ref[t] = 0
    for copy in copies:
        copy.wait()

    def place(i, carry):
        dest = dest_ref[i]
        rank = count_ref[dest]
        count_ref[dest] = rank + 1
        row = dest * (4 * cap) + rank
        out_ref[pl.ds(row, 1), :] = cell_ref[0, pl.ds(i, 1), :].astype(F32)
        out_ref[pl.ds(row + cap, 1), :] = offset_ref[0, 0, pl.ds(i, 1), :]
        out_ref[pl.ds(row + 2 * cap, 1), :] = offset_ref[0, 1, pl.ds(i, 1), :]
        out_ref[pl.ds(row + 3 * cap, 1), :] = mass_ref[0, pl.ds(i, 1), :]
        return carry

    lax.fori_loop(0, blocks, place, 0)


def deposit_kernel(in_ref, out_ref, acc_ref, *, scaling, tile_rows):
    tiles = in_ref.shape[0]
    cap = in_ref.shape[1] // 4
    lanes = in_ref.shape[2]
    group = min(8, cap)
    rows = -(-(tile_rows + 1) // 16) * 16
    acc_ref[...] = jnp.zeros(acc_ref.shape, F32)
    row_iota = lax.broadcasted_iota(jnp.int32, (rows, lanes), 0).astype(F32).astype(BF16)
    col_iota = (lax.broadcasted_iota(jnp.int32, (NG, lanes), 0) - NG // 2).astype(F32).astype(BF16)
    zero = jnp.zeros((), BF16)
    one = jnp.ones((), BF16)

    def step(src, start):
        pieces_r = []
        pieces_c = []
        for j in range(start, start + group):
            cell = in_ref[src, pl.ds(j, 1), :].astype(jnp.int32)
            frac_r = in_ref[src, pl.ds(cap + j, 1), :]
            frac_c = in_ref[src, pl.ds(2 * cap + j, 1), :]
            mass = in_ref[src, pl.ds(3 * cap + j, 1), :]
            row_id = (cell // NG).astype(F32)
            col_id = (cell % NG - NG // 2).astype(F32).astype(BF16)
            first = row_iota == row_id.astype(BF16)
            second = row_iota == (row_id + 1.0).astype(BF16)
            upper = mass * (1.0 - frac_r)
            lower = mass * frac_r
            rows_now = []
            for side in (1.0 - frac_c, frac_c):
                a_hi, a_lo = split(upper * side)
                b_hi, b_lo = split(lower * side)
                rows_now.append(jnp.where(first, a_hi, jnp.where(second, b_hi, zero)))
                rows_now.append(jnp.where(first, a_lo, jnp.where(second, b_lo, zero)))
            pieces_r.append(jnp.concatenate(rows_now, axis=0))
            pieces_c.append(jnp.where(col_iota == col_id, one, zero))
        acc_ref[...] += dot_nt(jnp.concatenate(pieces_r, axis=1), jnp.concatenate(pieces_c, axis=1))

    def per_source(src, carry):
        step(src, 0)
        for start in range(group, cap, group):
            block = in_ref[src, pl.ds(3 * cap + start, group), :]

            @pl.when(jnp.max(jnp.abs(block)) > 0.0)
            def _():
                step(src, start)

        return carry

    lax.fori_loop(0, tiles, per_source, 0)
    near = acc_ref[0:rows, :] + acc_ref[rows : 2 * rows, :]
    far = acc_ref[2 * rows : 3 * rows, :] + acc_ref[3 * rows : 4 * rows, :]
    lane = lax.broadcasted_iota(jnp.int32, (rows, NG), 1)
    total = (near + jnp.where(lane == 0, 0.0, pltpu.roll(far, 1, 1))) * scaling
    out_ref[...] = total[0 : out_ref.shape[0], :]


def unit_circle(left, right):
    turn = (left * right % NP).astype(F32) * WAVE
    return jnp.cos(turn), jnp.sin(turn)


def tables_kernel(v_hi_ref, v_lo_ref, u_hi_ref, u_lo_ref):
    lanes = 128
    fine = 32
    shape = (HALF // fine, lanes)
    coarse_c, coarse_s = unit_circle(
        fine * lax.broadcasted_iota(jnp.int32, shape, 0), lax.broadcasted_iota(jnp.int32, shape, 1)
    )
    shape = (fine, lanes)
    fine_c, fine_s = unit_circle(
        lax.broadcasted_iota(jnp.int32, shape, 0), lax.broadcasted_iota(jnp.int32, shape, 1)
    )
    parity = (1 - 2 * (lax.broadcasted_iota(jnp.int32, shape, 1) % 2)).astype(F32)
    first = lax.broadcasted_iota(jnp.int32, shape, 0) == 0
    for a in range(HALF // fine):
        ca = coarse_c[a : a + 1, :]
        sa = coarse_s[a : a + 1, :]
        base_cos = fine_c * ca - fine_s * sa
        base_sin = fine_s * ca + fine_c * sa
        k_index = a * fine + lax.broadcasted_iota(jnp.int32, shape, 0)
        for j in range(NG // lanes):
            q_cos, q_sin = 1.0, 0.0
            if j:
                step = NP // math.gcd(NP, lanes * j)
                turn = (k_index * (lanes * j)) % NP
                q_cos = jnp.ones(shape, F32)
                q_sin = jnp.zeros(shape, F32)
                for q in range(1, step):
                    angle = 2.0 * math.pi * q / step
                    hit = turn == q * (NP // step)
                    q_cos = jnp.where(hit, math.cos(angle), q_cos)
                    q_sin = jnp.where(hit, math.sin(angle), q_sin)
            cos_now = base_cos * q_cos - base_sin * q_sin
            sin_now = base_sin * q_cos + base_cos * q_sin
            if a == 0:
                sin_now = jnp.where(first, parity, sin_now)
            for at, value in ((0, cos_now), (HALF, sin_now)):
                hi, lo = split(value)
                v_hi_ref[at + a * fine : at + (a + 1) * fine, j * lanes : (j + 1) * lanes] = hi
                v_lo_ref[at + a * fine : at + (a + 1) * fine, j * lanes : (j + 1) * lanes] = lo
    win = u_hi_ref.shape[0] // 2
    fine = 16
    shape = (fine, HALF)
    fine_c, fine_s = unit_circle(
        lax.broadcasted_iota(jnp.int32, shape, 0), lax.broadcasted_iota(jnp.int32, shape, 1)
    )
    lane = lax.broadcasted_iota(jnp.int32, shape, 1)
    wave = lane.astype(F32) * WAVE
    parity = (1 - 2 * (lax.broadcasted_iota(jnp.int32, shape, 0) % 2)).astype(F32)
    for a in range(win // fine):
        ca, sa = unit_circle(jnp.full((1, HALF), a * fine, jnp.int32), lane[0:1])
        w_cos = fine_c * ca - fine_s * sa
        w_sin = fine_s * ca + fine_c * sa
        for rows, cols, value in (
            (0, 0, w_cos),
            (0, HALF, jnp.where(lane == 0, parity, w_sin)),
            (win, 0, -wave * w_sin),
            (win, HALF, wave * w_cos),
        ):
            hi, lo = split(value)
            u_hi_ref[rows + a * fine : rows + (a + 1) * fine, cols : cols + HALF] = hi
            u_lo_ref[rows + a * fine : rows + (a + 1) * fine, cols : cols + HALF] = lo


def fields_kernel(
    mine_ref,
    other_ref,
    v_hi_ref,
    v_lo_ref,
    u_hi_ref,
    u_lo_ref,
    lens_ref,
    tab_ref,
    ba_ref,
    window_ref,
    corner_ref,
    dens_ref,
    dens_hi_ref,
    dens_lo_ref,
    l_hi_ref,
    l_lo_ref,
    *,
    tile_rows,
):
    tile = lax.axis_index("tile")
    parity = tile % 2
    pairs = mine_ref.shape[0]
    tiles = 2 * pairs
    win = 3 * tile_rows
    pad = tile_rows
    zeros = jnp.zeros((pad, NG), F32)
    dens_ref[0:pad, :] = zeros
    dens_ref[pad + NG : pad + NG + pad, :] = zeros
    for half, src in ((0, mine_ref), (1, other_ref)):
        for j in range(pairs):
            t = 2 * j + jnp.bitwise_xor(parity, half)
            row = pl.multiple_of(pad + t * tile_rows, 8)
            dens_ref[pl.ds(row, tile_rows), :] = src[j, 0:tile_rows, :]
    for half, src in ((0, mine_ref), (1, other_ref)):
        for j in range(pairs):
            t = 2 * j + jnp.bitwise_xor(parity, half)
            row = pl.multiple_of(pad + (t + 1) * tile_rows, 8)
            spill = jnp.where(t + 1 < tiles, src[j, tile_rows : tile_rows + 8, :], 0.0)
            dens_ref[pl.ds(row, 8), :] += spill
    d_hi, d_lo = split(dens_ref[pad : pad + NG, :])
    dens_hi_ref[...] = d_hi
    dens_lo_ref[...] = d_lo

    half_lane = lax.broadcasted_iota(jnp.int32, (1, HALF), 1).astype(F32) * WAVE
    origin = (tile - 1) * tile_rows + NP
    turn = (lax.broadcasted_iota(jnp.int32, (1, HALF), 1) * origin % NP).astype(F32) * WAVE
    turn_cos = jnp.cos(turn)
    turn_sin = jnp.sin(turn)
    lane = lax.broadcasted_iota(jnp.int32, (1, NP), 1)
    k_slot = jnp.where(lane < HALF, lane, jnp.where(lane == HALF, HALF, lane - HALF))
    kx = k_slot.astype(F32) * WAVE
    kx2 = kx * kx
    edge_k = (lane == 0) | (lane == HALF)
    weight_k = jnp.where(edge_k, 1.0, 2.0)
    block = 256

    def channel_block(i, corner):
        at = pl.multiple_of(i * block, block)
        v_hi = v_hi_ref[pl.ds(at, block), :]
        v_lo = v_lo_ref[pl.ds(at, block), :]
        dh = dens_hi_ref[...]
        first = dot_nt(v_hi, dh) + dot_nt(v_lo, dh) + dot_nt(v_hi, dens_lo_ref[...])
        f_hi, f_lo = split(first)
        spec = (
            dot_nt(f_hi, v_hi_ref[...]) + dot_nt(f_lo, v_hi_ref[...]) + dot_nt(f_hi, v_lo_ref[...])
        )
        chan = at + lax.broadcasted_iota(jnp.int32, (block, 1), 0)
        l_slot = jnp.where(chan < HALF, chan, jnp.where(chan == HALF, HALF, chan - HALF))
        ky = l_slot.astype(F32) * WAVE
        weight_l = jnp.where((chan == 0) | (chan == HALF), 1.0, 2.0)
        scale = (weight_l * (-2.0 / (NP * NP))) * weight_k
        pot = spec * (scale / (kx2 + ky * ky + MU2))
        corner = jnp.where(i == HALF // block, pot[0:1, HALF : HALF + 1], corner)
        pot_c = pot[:, 0:HALF]
        pot_s = pot[:, HALF:NP]
        turned = jnp.concatenate(
            [pot_c * turn_cos + pot_s * turn_sin, pot_s * turn_cos - pot_c * turn_sin], axis=1
        )
        p_hi, p_lo = split(turned)
        uh = u_hi_ref[...]
        ba_ref[:, pl.ds(at, block)] = (
            dot_nt(uh, p_hi) + dot_nt(u_lo_ref[...], p_hi) + dot_nt(uh, p_lo)
        )
        return corner

    corner = lax.fori_loop(0, NP // block, channel_block, jnp.zeros((1, 1), F32))

    row_at = lax.broadcasted_iota(jnp.int32, (win, 1), 0)
    grid_row = (tile - 1) * tile_rows + row_at
    inside = ((grid_row >= 0) & (grid_row < NG)).astype(F32)
    b_all = ba_ref[0:win, :] * inside
    a_all = ba_ref[win : 2 * win, :] * inside
    ba_ref[0:win, :] = b_all
    ba_ref[win : 2 * win, :] = a_all
    window_ref[...] = dens_ref[pl.ds(pl.multiple_of(tile * tile_rows, 8), win), :]
    corner_ref[...] = jnp.broadcast_to(corner * (-math.pi * math.pi), corner_ref.shape)
    slope = jnp.concatenate([half_lane * b_all[:, HALF:NP], -half_lane * b_all[:, 0:HALF]], axis=1)
    for f, value in enumerate((a_all, slope)):
        hi, lo = split(value)
        l_hi_ref[f * win : (f + 1) * win, :] = hi
        l_lo_ref[f * win : (f + 1) * win, :] = lo
    finish(2, l_hi_ref, l_lo_ref, v_hi_ref, v_lo_ref, None, lens_ref, tab_ref, tile_rows)


def finish(count, l_hi_ref, l_lo_ref, v_hi_ref, v_lo_ref, extra_ref, lens_ref, tab_ref, tile_rows):
    win = 3 * tile_rows
    shape = (win // SUB, SUB, NG)
    vh = v_hi_ref[...]
    out = dot_nn(l_hi_ref[...], vh) + dot_nn(l_lo_ref[...], vh) + dot_nn(l_hi_ref[...], v_lo_ref[...])
    at = lens_ref.shape[-3] - count
    for f in range(count):
        value = out[f * win : (f + 1) * win, :]
        if f == 0 and extra_ref is not None:
            value = value + 2.0 * extra_ref[...]
        lens_ref[..., at + f, :, :] = value[tile_rows : 2 * tile_rows, :].reshape(
            (1,) * (len(lens_ref.shape) - 3) + (tile_rows, NG)
        )
        hi, lo = split(value)
        tab_ref[:, f, :, 0:NG] = hi.reshape(shape)
        tab_ref[:, f, :, NG : 2 * NG] = lo.reshape(shape)
        tab_ref[:, f, :, 2 * NG : 3 * NG] = hi.reshape(shape)


def second_kernel(
    ba_ref,
    window_ref,
    corner_ref,
    part_ref,
    v_hi_ref,
    v_lo_ref,
    lens_ref,
    tab_ref,
    l_hi_ref,
    l_lo_ref,
    *,
    tile_rows,
):
    tile = lax.axis_index("tile")
    win = 3 * tile_rows
    lens_ref[0, 0:2] = part_ref[...]
    row_at = lax.broadcasted_iota(jnp.int32, (win, 1), 0)
    grid_row = (tile - 1) * tile_rows + row_at
    inside = ((grid_row >= 0) & (grid_row < NG)).astype(F32)
    corner_col = inside * (1 - 2 * (row_at % 2)).astype(F32) * corner_ref[0:1, 0:1]
    lane = lax.broadcasted_iota(jnp.int32, (1, NP), 1)
    slot = jnp.where(lane < HALF, lane, jnp.where(lane == HALF, HALF, lane - HALF))
    ky2 = (slot.astype(F32) * WAVE) * (slot.astype(F32) * WAVE)
    lane_half = lax.broadcasted_iota(jnp.int32, (1, HALF), 1)
    half_lane = lane_half.astype(F32) * WAVE
    b_all = ba_ref[0:win, :]
    a_cos = ba_ref[win : 2 * win, 0:HALF]
    a_sin = ba_ref[win : 2 * win, HALF:NP]
    mixed = jnp.concatenate(
        [half_lane * a_sin, jnp.where(lane_half == 0, corner_col, -half_lane * a_cos)], axis=1
    )
    for f, value in enumerate(((MU2 + ky2) * b_all, mixed, -ky2 * b_all)):
        hi, lo = split(value)
        l_hi_ref[f * win : (f + 1) * win, :] = hi
        l_lo_ref[f * win : (f + 1) * win, :] = lo
    finish(3, l_hi_ref, l_lo_ref, v_hi_ref, v_lo_ref, window_ref, lens_ref, tab_ref, tile_rows)


def lookup(geo_ref, tab_ref, emit):
    chunks, fields, _, _ = tab_ref.shape
    group = geo_ref.shape[0] // 4
    rays = geo_ref.shape[1]
    n = min(RAY_CHUNK, rays)
    per = rays // n
    zero = jnp.zeros((), BF16)
    win = chunks * SUB
    least = float(win)
    most = 0.0
    for g in range(group):
        row_id = geo_ref[4 * g : 4 * g + 1, :]
        least = jnp.minimum(least, jnp.min(row_id))
        most = jnp.maximum(most, jnp.max(row_id))
    low = jnp.clip(least.astype(jnp.int32), 0, win - 1) // SUB
    high = jnp.clip(most.astype(jnp.int32) + 1, 0, win - 1) // SUB
    needed = high - low + 1
    tiers = sorted({min(t, chunks) for t in TIERS})

    def with_tier(tier, passes):
        col_iota = (lax.broadcasted_iota(jnp.int32, (NG, n), 0) - NG // 2).astype(F32).astype(BF16)
        row_iota = lax.broadcasted_iota(jnp.int32, (tier * SUB, n), 0).astype(F32)

        def chunk(i, carry):
            g = i // per
            at = pl.multiple_of((i % per) * n, n)
            row_id = geo_ref[pl.ds(4 * g, 1), pl.ds(at, n)]
            frac_row = geo_ref[pl.ds(4 * g + 1, 1), pl.ds(at, n)]
            col_floor = geo_ref[pl.ds(4 * g + 2, 1), pl.ds(at, n)]
            frac_col = geo_ref[pl.ds(4 * g + 3, 1), pl.ds(at, n)]
            far = 4.0 * NG
            c0 = jnp.where((col_floor >= 0.0) & (col_floor < NG), col_floor - NG // 2, far)
            c1 = jnp.where(
                (col_floor >= -1.0) & (col_floor < NG - 1.0), col_floor + (1.0 - NG // 2), far
            )
            here = col_iota == c0.astype(BF16)
            there = col_iota == c1.astype(BF16)
            g0_hi, g0_lo = split(1.0 - frac_col)
            g1_hi, g1_lo = split(frac_col)
            w_hi = jnp.where(here, g0_hi, jnp.where(there, g1_hi, zero))
            w_lo = jnp.where(here, g0_lo, jnp.where(there, g1_lo, zero))
            w = jnp.concatenate([w_hi, w_hi, w_lo], axis=0)

            def rows_from(start, floor):
                here_row = row_id - (start * SUB).astype(F32)
                row_w = jnp.where(row_iota == here_row, 1.0 - frac_row, 0.0) + jnp.where(
                    row_iota == here_row + 1.0, frac_row, 0.0
                )
                if floor is not None:
                    row_w = jnp.where(row_iota >= floor, row_w, 0.0)
                table = tab_ref[pl.ds(start, tier)].reshape(tier * fields * SUB, 3 * NG)
                along = dot_nn(table, w).reshape(tier, fields, SUB, n)
                values = jnp.sum(along * row_w.reshape(tier, 1, SUB, n), axis=0)
                return jnp.sum(values, axis=1)

            if passes == 1:
                values = rows_from(jnp.minimum(low, chunks - tier), None)
            else:

                def one_pass(q, total):
                    start = jnp.minimum(q * tier, chunks - tier)
                    return total + rows_from(start, ((q * tier - start) * SUB).astype(F32))

                values = lax.fori_loop(0, passes, one_pass, jnp.zeros((fields, n), F32))
            emit(g, at, n, values)
            return carry

        lax.fori_loop(0, group * per, chunk, 0)

    floor = 0
    for tier in tiers:
        pl.when((needed > floor) & (needed <= tier))(lambda tier=tier: with_tier(tier, 1))
        floor = tier
    if floor < chunks:
        pl.when(needed > floor)(lambda: with_tier(4, -(-chunks // 4)))


def bent(plane, inbox_a, hess):
    rows = []
    for i in range(hess.shape[0] // 3):
        hxx = hess[3 * i : 3 * i + 1]
        hxy = hess[3 * i + 1 : 3 * i + 2]
        hyy = hess[3 * i + 2 : 3 * i + 3]
        first = plane == 0
        a11, a12, a21, a22 = (
            jnp.where(first, start, inbox_a[4 * i + c : 4 * i + c + 1])
            for c, start in enumerate((1.0, 0.0, 0.0, 1.0))
        )
        rows += [
            a11 - LENS_WEIGHT * (hxx * a11 + hxy * a21),
            a12 - LENS_WEIGHT * (hxx * a12 + hxy * a22),
            a21 - LENS_WEIGHT * (hxy * a11 + hyy * a21),
            a22 - LENS_WEIGHT * (hxy * a12 + hyy * a22),
        ]
    return jnp.concatenate(rows, axis=0)


def move_kernel(*refs, tile_rows, turn):
    if turn:
        inbox_ref, inbox_a_ref, hess_ref, cell_ref, offset_ref, tab_ref, out_ref, bend_ref, geo_ref = refs
    else:
        cell_ref, offset_ref, tab_ref, out_ref, geo_ref = refs
    tile = lax.axis_index("tile")
    plane = lax.axis_index("plane")
    group = geo_ref.shape[0] // 4
    groups = cell_ref.shape[0] // group
    which = turn - plane
    active = (which >= 0) & (which < groups)
    span = float(tile_rows - 1)
    if turn:
        bend_ref[...] = bent(plane, inbox_a_ref[...], hess_ref[...])

    def came(g, axis, at, n):
        if not turn:
            return jnp.zeros((1, n), F32)
        return jnp.where(plane == 0, 0.0, inbox_ref[pl.ds(2 * g + axis, 1), pl.ds(at, n)])

    @pl.when(active)
    def _():
        rays = out_ref.shape[1]
        for g in range(group):
            batch = which * group + g
            cell = cell_ref[pl.ds(batch, 1), :]
            base_row = (tile * tile_rows + cell // NG).astype(F32) + offset_ref[0, pl.ds(batch, 1), :]
            base_col = (cell % NG).astype(F32) + offset_ref[1, pl.ds(batch, 1), :]
            row_pos = base_row + span * jnp.tanh(came(g, 0, 0, rays) / span)
            col_pos = base_col + span * jnp.tanh(came(g, 1, 0, rays) / span)
            row_floor = jnp.floor(row_pos)
            col_floor = jnp.floor(col_pos)
            geo_ref[4 * g : 4 * g + 1, :] = row_floor - ((tile - 1) * tile_rows).astype(F32)
            geo_ref[4 * g + 1 : 4 * g + 2, :] = row_pos - row_floor
            geo_ref[4 * g + 2 : 4 * g + 3, :] = col_floor
            geo_ref[4 * g + 3 : 4 * g + 4, :] = col_pos - col_floor

        def emit(g, at, n, values):
            for axis in (0, 1):
                out_ref[pl.ds(2 * g + axis, 1), pl.ds(at, n)] = (
                    came(g, axis, at, n) - LENS_WEIGHT * values[axis : axis + 1]
                )

        lookup(geo_ref, tab_ref, emit)

    @pl.when(jnp.logical_not(active))
    def _():
        out_ref[...] = jnp.zeros(out_ref.shape, F32)
        geo_ref[...] = jnp.zeros(geo_ref.shape, F32)


def hessian_kernel(geo_ref, tab_ref, out_ref, *, groups, turn):
    which = turn - lax.axis_index("plane")
    active = (which >= 0) & (which < groups)

    @pl.when(active)
    def _():
        def emit(g, at, n, values):
            for c in range(3):
                out_ref[pl.ds(3 * g + c, 1), pl.ds(at, n)] = values[c : c + 1]

        lookup(geo_ref, tab_ref, emit)

    @pl.when(jnp.logical_not(active))
    def _():
        out_ref[...] = jnp.zeros(out_ref.shape, F32)


def gather_kernel(*refs, planes, turns):
    pos_refs = refs[0:turns]
    bend_refs = refs[turns : 2 * turns - 1]
    inbox_a_ref, hess_ref, out_ref = refs[2 * turns - 1 :]
    plane = lax.axis_index("plane")
    group = hess_ref.shape[0] // 3
    groups = out_ref.shape[1] // group
    for p in range(planes):

        @pl.when(plane == p)
        def _():
            for j in range(groups):
                if p + j < len(bend_refs):
                    late = bend_refs[p + j][...]
                else:
                    late = bent(plane, inbox_a_ref[...], hess_ref[...])
                for i in range(group):
                    out_ref[0, j * group + i, 0:2, :] = pos_refs[p + j][2 * i : 2 * i + 2, :]
                    out_ref[0, j * group + i, 2:6, :] = late[4 * i : 4 * i + 4, :]


def per_device(block_dest, particle_cell, particle_offset, particle_mass, ray_cell, ray_offset):
    tiles = lax.axis_size("tile")
    planes = lax.axis_size("plane")
    tile_rows = NG // tiles
    tile_now = lax.axis_index("tile")
    plane_now = lax.axis_index("plane")
    blocks = particle_cell.shape[1]
    block_len = particle_cell.shape[2]
    cap = 2 * blocks // tiles
    win = 3 * tile_rows

    outgoing = pl.pallas_call(
        route_kernel,
        out_shape=jax.ShapeDtypeStruct((tiles * 4 * cap, block_len), F32),
        in_specs=[hbm_spec()] * 4,
        out_specs=vmem_spec(),
        scratch_shapes=[
            pltpu.SMEM((blocks,), jnp.int32),
            VMEM(particle_cell.shape, jnp.int32),
            VMEM(particle_offset.shape, F32),
            VMEM(particle_mass.shape, F32),
            pltpu.SMEM((tiles,), jnp.int32),
            pltpu.SemaphoreType.DMA((4,)),
        ],
        compiler_params=params(58),
        name="route",
    )(block_dest.reshape(-1), particle_cell, particle_offset, particle_mass)
    incoming = lax.all_to_all(
        outgoing.reshape(tiles, 4 * cap, block_len), "tile", split_axis=0, concat_axis=0, tiled=True
    )

    v_hi, v_lo, u_hi, u_lo = pl.pallas_call(
        tables_kernel,
        out_shape=(
            jax.ShapeDtypeStruct((NP, NG), BF16),
            jax.ShapeDtypeStruct((NP, NG), BF16),
            jax.ShapeDtypeStruct((2 * win, NP), BF16),
            jax.ShapeDtypeStruct((2 * win, NP), BF16),
        ),
        in_specs=[],
        out_specs=(vmem_spec(),) * 4,
        compiler_params=params(12),
        name="tables",
    )()

    scaling = math.sqrt(tile_rows * NG / (BLOCKS_DEV * block_len))
    rows_acc = -(-(tile_rows + 1) // 16) * 16
    canvas_rows = tile_rows + 8
    canvas = pl.pallas_call(
        lambda a, b, c: deposit_kernel(a, b, c, scaling=scaling, tile_rows=tile_rows),
        out_shape=jax.ShapeDtypeStruct((canvas_rows, NG), F32),
        in_specs=[vmem_spec()],
        out_specs=vmem_spec(),
        scratch_shapes=[VMEM((4 * rows_acc, NG), F32)],
        compiler_params=params(12),
        name="deposit",
    )(incoming)

    groups = [[i for i in range(tiles) if i % 2 == p] for p in (0, 1)]
    mine = lax.all_gather(canvas, "tile", axis=0, tiled=False, axis_index_groups=groups)
    other = lax.ppermute(mine, "tile", [(i, i ^ 1) for i in range(tiles)])

    shape = jax.ShapeDtypeStruct
    part, tab_a, ba, window, corner = pl.pallas_call(
        lambda *refs: fields_kernel(*refs, tile_rows=tile_rows),
        out_shape=(
            shape((2, tile_rows, NG), F32),
            shape((win // SUB, 2, SUB, 3 * NG), BF16),
            shape((2 * win, NP), F32),
            shape((win, NG), F32),
            shape((8, 128), F32),
        ),
        in_specs=[vmem_spec()] * 6,
        out_specs=(vmem_spec(),) * 5,
        scratch_shapes=[
            VMEM((NG + 2 * tile_rows, NG), F32),
            VMEM((NG, NG), BF16),
            VMEM((NG, NG), BF16),
            VMEM((2 * win, NP), BF16),
            VMEM((2 * win, NP), BF16),
        ],
        compiler_params=params(24),
        name="fields",
    )(mine, other, v_hi, v_lo, u_hi, u_lo)
    lens, tab_h = pl.pallas_call(
        lambda *refs: second_kernel(*refs, tile_rows=tile_rows),
        out_shape=(
            shape((1, 5, tile_rows, NG), F32),
            shape((win // SUB, 3, SUB, 3 * NG), BF16),
        ),
        in_specs=[vmem_spec()] * 6,
        out_specs=(vmem_spec(),) * 2,
        scratch_shapes=[VMEM((3 * win, NP), BF16), VMEM((3 * win, NP), BF16)],
        compiler_params=params(16),
        name="second",
    )(ba, window, corner, part, v_hi, v_lo)

    batches = ray_cell.shape[0]
    rays = ray_cell.shape[1]
    groups_b = batches // GROUP
    ring = [(i, (i + 1) % planes) for i in range(planes)]
    turns = groups_b + planes - 1
    received = ()
    positions = []
    bends = []
    inbox_a = jnp.zeros((4 * GROUP, rays), F32)
    for turn in range(turns):
        out_shape = [shape((2 * GROUP, rays), F32), shape((4 * GROUP, rays), F32)]
        if turn:
            out_shape.append(shape((4 * GROUP, rays), F32))
        moved = pl.pallas_call(
            lambda *refs, turn=turn: move_kernel(*refs, tile_rows=tile_rows, turn=turn),
            out_shape=tuple(out_shape),
            in_specs=[vmem_spec()] * (len(received) + 3),
            out_specs=(vmem_spec(),) * len(out_shape),
            compiler_params=params(16),
            name=f"move{turn}",
        )(*received, ray_cell, ray_offset, tab_a)
        positions.append(moved[0])
        inbox = None
        if turn < turns - 1:
            inbox = lax.ppermute(moved[0], "plane", ring)
        if turn:
            bends.append(moved[1])
            inbox_a = lax.ppermute(moved[1], "plane", ring)
        hess = pl.pallas_call(
            lambda *refs, turn=turn: hessian_kernel(*refs, groups=groups_b, turn=turn),
            out_shape=shape((3 * GROUP, rays), F32),
            in_specs=[vmem_spec()] * 2,
            out_specs=vmem_spec(),
            compiler_params=params(16),
            name=f"hessian{turn}",
        )(moved[-1], tab_h)
        received = (inbox, inbox_a, hess)
    ray_maps = pl.pallas_call(
        lambda *refs: gather_kernel(*refs, planes=planes, turns=turns),
        out_shape=shape((1, batches, 6, rays), F32),
        in_specs=[vmem_spec()] * (2 * turns + 1),
        out_specs=vmem_spec(),
        compiler_params=params(8),
        name="gather",
    )(*positions, *bends, inbox_a, received[2])
    return (lens, ray_maps)


def solution(mesh):
    return jax.shard_map(
        per_device,
        mesh=mesh,
        in_specs=(
            P("plane", "tile", None),
            P("plane", "tile", None),
            P("plane", None, "tile", None),
            P("plane", "tile", None),
            P(None, "tile"),
            P(None, None, "tile"),
        ),
        out_specs=(P("plane", None, "tile", None), P("plane", None, None, "tile")),
        check_vma=False,
    )
```

time: 162 us -> 98.9 us (0.61)
  the two profiles are of different devices: /device:TPU:26 before, /device:TPU:0 now
where the time goes in v2:
time: 98.9 us; the launch traced here: 98.3 us
  Pallas kernels  44.7 us (45%)
  blocking collectives  23.7 us (24%)
  waiting for transfers between devices  15.2 us (15%)
  starting transfers between devices  13.1 us (13%)
    all_to_all x1, blocking collectives, per_device(): lax.all_to_all(outgoing.reshape(tiles, 4 * cap, block_len), 'tile', split...  12.1 us
    all_gather x1, blocking collectives, per_device(): lax.all_gather(canvas, 'tile', axis=0, tiled=False, axis_index_groups=gro...  11.6 us
    pallas_call x1, Pallas kernels, per_device(): pl.pallas_call(lambda *refs: fields_kernel(*refs, tile_rows=tile_rows), o...  11.4 us
    pallas_call x5, Pallas kernels, per_device(): pl.pallas_call(lambda *refs, turn=turn: hessian_kernel(*refs, groups=grou...  10.2 us
    pallas_call x5, Pallas kernels, per_device(): pl.pallas_call(lambda *refs, turn=turn: move_kernel(*refs, tile_rows=tile...  8.51 us
    ppermute x4, waiting for transfers between devices, per_device(): inbox = lax.ppermute(moved[0], 'plane', ring)  8.11 us
    ppermute x4, waiting for transfers between devices, per_device(): inbox_a = lax.ppermute(moved[1], 'plane', ring)  7.11 us
    pallas_call x1, Pallas kernels, per_device(): pl.pallas_call(lambda a, b, c: deposit_kernel(a, b, c, scaling=scaling, t...  6.93 us
  transfers between devices with their start and end apart: 9, of which 4 were waited for; matrix products, arithmetic and copies ran while one was open for 0% of the time, Pallas kernels for 16%

profile of v2, /device:TPU:0, one launch (start us, length us, event | category | flops | bytes accessed | tf_op | source)
XLA Modules:
  0.0 98.3 jit_solution(2163454870893260951)
XLA Ops:
  0.6 2.2 %route.1 = f32[512,128]{1,0:T(8,128)} custom-call(s32[64]{0:T(128)} %bitcast.6, s32[1,64,128]{2,1,0:T(8,128)} %cell_hbm.1, f32[1,2,64,128]{3,2,1,0:T(8,128)} %offset_hbm.1, f32[1,64,128]{2,1,0:T(8,128)} %mass_hbm.1), custom_call_target="tpu_custom_call" | custom-call | tf_op jit(solution)/shard_map/route/pallas_call | solution.py:577
  2.8 12.1 %all_to_all.5.a = f32[8,64,128]{2,1,0:T(8,128)S(1)} all-to-all(f32[8,64,128]{2,1,0:T(8,128)} %bitcast.5), channel_id=1, replica_groups=mesh['plane'=4,'tile'=8] {'tile'}, dimensions={0} | all-to-all | bytes 524288 | tf_op jit(solution)/shard_map/all_to_all | solution.py:593
  14.9 6.9 %deposit.1 = f32[72,512]{1,0:T(8,128)S(1)} custom-call(f32[8,64,128]{2,1,0:T(8,128)S(1)} %all_to_all.5.a), custom_call_target="tpu_custom_call" | custom-call | tf_op jit(solution)/shard_map/deposit/pallas_call | solution.py:614
  21.8 11.6 %all-gather = f32[288,512]{1,0:T(8,128)S(1)} all-gather(f32[72,512]{1,0:T(8,128)S(1)} %deposit.1), channel_id=2, replica_groups={{0,2,4,6},{1,3,5,7},{8,10,12,14},{9,11,13,15},{16,18,20,22},{17,19,21,2..., dimensions={0}, use_global_device_ids=true | all-gather | bytes 737280 | tf_op jit(solution)/shard_map/all_gather | solution.py:625
  33.4 0.0 collective-permute-start
  33.4 2.5 %tables.1 = (bf16[1024,512]{1,0:T(8,128)(2,1)S(1)}, bf16[1024,512]{1,0:T(8,128)(2,1)S(1)}, bf16[384,1024]{1,0:T(8,128)(2,1)S(1)}, bf16[384,1024]{1,0:T(8,128)(2,1)S(1)}) custom-call(), custom_call_target="tpu_custom_call" | custom-call | tf_op jit(solution)/shard_map/tables/pallas_call | solution.py:597
  36.0 0.0 collective-permute-done.refs_1_
  36.0 0.0 copy-start
  36.0 0.0 copy-start.1
  36.0 11.4 %fields.1 = (f32[2,64,512]{2,1,0:T(8,128)S(1)}, bf16[12,2,16,1536]{3,2,1,0:T(8,128)(2,1)S(1)}, f32[384,1024]{1,0:T(8,128)S(1)}, f32[192,512]{1,0:T(8,128)S(1)}, f32[8,128]{1,0:T(8,128)S(1)}) custom-call(f32[4,72,512]{2,1,0:T(8,128)S(1)} %bitcast.4, f32[4,72,512]{2,1,0:T(8,128)S(1)} %collective-permute-done.refs_1_, ...), custom_call_target="tpu_custom_call" | custom-call | tf_op jit(solution)/shard_map/fields/pallas_call | solution.py:629
  47.4 0.0 copy-done
  47.4 0.0 copy-done.1
  47.4 4.0 %move0.1 = (f32[4,2048]{1,0:T(4,128)S(1)}, f32[8,2048]{1,0:T(8,128)S(1)}) custom-call(s32[4,2048]{1,0:T(4,128)S(1)} %copy-done.1, f32[2,4,2048]{2,1,0:T(4,128)S(1)} %copy-done, bf16[12,2,16,1536]{3,2,1,0:T(8,128)(2,1)S(1)} %get-tuple-element.36.refs_2_.refs_5_), custom_call_target="tpu_custom_call" | custom-call | tf_op jit(solution)/shard_map/move0/pallas_call | solution.py:676
  51.4 0.1 collective-permute-start.1
  51.5 2.9 %second.1 = (f32[1,5,64,512]{3,2,1,0:T(8,128)}, bf16[12,3,16,1536]{3,2,1,0:T(8,128)(2,1)S(1)}) custom-call(f32[384,1024]{1,0:T(8,128)S(1)} %get-tuple-element.31.refs_0_, f32[192,512]{1,0:T(8,128)S(1)} %get-tuple-element.32.refs_1_, f32[8,128]{1,0:T(8,128)S(1)} %get-tuple-element.33.refs_2_, f32[2,64,512]{2,1,0:T(8,128)S(1)} %get-tuple-element.34.refs_3_, ...), custom_call_target="tpu_custom_call" | custom-call | tf_op jit(solution)/shard_map/second/pallas_call | solution.py:650
  54.4 5.2 %hessian0.1.refs_2_ = f32[6,2048]{1,0:T(8,128)S(1)} custom-call(f32[8,2048]{1,0:T(8,128)S(1)} %get-tuple-element.38.refs_0_, bf16[12,3,16,1536]{3,2,1,0:T(8,128)(2,1)S(1)} %get-tuple-element.39.refs_1_), custom_call_target="tpu_custom_call" | custom-call | tf_op jit(solution)/shard_map/hessian0/pallas_call | solution.py:691
  59.6 0.0 collective-permute-done.1.refs_0_
  59.6 4.1 %move1.1 = (f32[4,2048]{1,0:T(4,128)S(1)}, f32[8,2048]{1,0:T(8,128)S(1)}, f32[8,2048]{1,0:T(8,128)S(1)}) custom-call(f32[4,2048]{1,0:T(4,128)S(1)} %collective-permute-done.1.refs_0_, f32[8,2048]{1,0:T(8,128)S(1)} %broadcast_in_dim.3.refs_1_, f32[6,2048]{1,0:T(8,128)S(1)} %hessian0.1.refs_2_, s32[4,2048]{1,0:T(4,128)S(1)} %copy-done.1, ...), custom_call_target="tpu_custom_call" | custom-call | tf_op jit(solution)/shard_map/move1/pallas_call | solution.py:676
  63.7 0.1 collective-permute-start.3
  63.8 0.1 collective-permute-start.2
  63.8 5.0 %hessian1.1.refs_2_ = f32[6,2048]{1,0:T(8,128)S(1)} custom-call(f32[8,2048]{1,0:T(8,128)S(1)} %get-tuple-element.42.refs_0_, bf16[12,3,16,1536]{3,2,1,0:T(8,128)(2,1)S(1)} %get-tuple-element.39.refs_1_), custom_call_target="tpu_custom_call" | custom-call | tf_op jit(solution)/shard_map/hessian1/pallas_call | solution.py:691
  68.9 1.9 %collective-permute-done.2.refs_0_ = f32[4,2048]{1,0:T(4,128)S(1)} collective-permute-done((f32[4,2048]{1,0:T(4,128)S(1)}, f32[4,2048]{1,0:T(4,128)S(1)}, u32[]{:S(2)}, u32[]{:S(2)}) %collective-permute-start.2) | collective-permute-done | bytes 32800 | tf_op jit(solution)/shard_map/ppermute | solution.py:687
  70.8 0.0 collective-permute-done.3.refs_1_
  70.8 0.1 move2.1
  70.9 3.0 %collective-permute-start.5 = (f32[8,2048]{1,0:T(8,128)S(1)}, f32[8,2048]{1,0:T(8,128)S(1)}, u32[]{:S(2)}, u32[]{:S(2)}) collective-permute-start(f32[8,2048]{1,0:T(8,128)S(1)} %get-tuple-element.44.refs_6_), channel_id=1, source_target_pairs={{0,8},{8,16},{16,24},{24,0},{1,9},{9,17},{17,25},{25,1},{2,10},{10... | collective-permute-start | bytes 196616 | tf_op jit(solution)/shard_map/ppermute | solution.py:690
  73.9 1.1 %collective-permute-start.4 = (f32[4,2048]{1,0:T(4,128)S(1)}, f32[4,2048]{1,0:T(4,128)S(1)}, u32[]{:S(2)}, u32[]{:S(2)}) collective-permute-start(f32[4,2048]{1,0:T(4,128)S(1)} %get-tuple-element.43.refs_2_), channel_id=1, source_target_pairs={{0,8},{8,16},{16,24},{24,0},{1,9},{9,17},{17,25},{25,1},{2,10},{10... | collective-permute-start | bytes 98312 | tf_op jit(solution)/shard_map/ppermute | solution.py:687
  75.0 4.6 %collective-permute-done.4.refs_0_ = f32[4,2048]{1,0:T(4,128)S(1)} collective-permute-done((f32[4,2048]{1,0:T(4,128)S(1)}, f32[4,2048]{1,0:T(4,128)S(1)}, u32[]{:S(2)}, u32[]{:S(2)}) %collective-permute-start.4) | collective-permute-done | bytes 32800 | tf_op jit(solution)/shard_map/ppermute | solution.py:687
  79.6 0.0 collective-permute-done.5.refs_1_
  79.6 0.1 move3.1
  79.7 1.2 %collective-permute-start.7 = (f32[8,2048]{1,0:T(8,128)S(1)}, f32[8,2048]{1,0:T(8,128)S(1)}, u32[]{:S(2)}, u32[]{:S(2)}) collective-permute-start(f32[8,2048]{1,0:T(8,128)S(1)} %get-tuple-element.47.refs_7_), channel_id=1, source_target_pairs={{0,8},{8,16},{16,24},{24,0},{1,9},{9,17},{17,25},{25,1},{2,10},{10... | collective-permute-start | bytes 196616 | tf_op jit(solution)/shard_map/ppermute | solution.py:690
  80.9 5.4 %collective-permute-start.6 = (f32[4,2048]{1,0:T(4,128)S(1)}, f32[4,2048]{1,0:T(4,128)S(1)}, u32[]{:S(2)}, u32[]{:S(2)}) collective-permute-start(f32[4,2048]{1,0:T(4,128)S(1)} %get-tuple-element.46.refs_3_), channel_id=1, source_target_pairs={{0,8},{8,16},{16,24},{24,0},{1,9},{9,17},{17,25},{25,1},{2,10},{10... | collective-permute-start | bytes 98312 | tf_op jit(solution)/shard_map/ppermute | solution.py:687
  86.3 1.6 %collective-permute-done.6.refs_0_ = f32[4,2048]{1,0:T(4,128)S(1)} collective-permute-done((f32[4,2048]{1,0:T(4,128)S(1)}, f32[4,2048]{1,0:T(4,128)S(1)}, u32[]{:S(2)}, u32[]{:S(2)}) %collective-permute-start.6) | collective-permute-done | bytes 32800 | tf_op jit(solution)/shard_map/ppermute | solution.py:687
  87.9 0.0 collective-permute-done.7.refs_1_
  87.9 0.1 move4.1
  88.0 2.4 %collective-permute-start.8 = (f32[8,2048]{1,0:T(8,128)S(1)}, f32[8,2048]{1,0:T(8,128)S(1)}, u32[]{:S(2)}, u32[]{:S(2)}) collective-permute-start(f32[8,2048]{1,0:T(8,128)S(1)} %get-tuple-element.50.refs_8_), channel_id=1, source_target_pairs={{0,8},{8,16},{16,24},{24,0},{1,9},{9,17},{17,25},{25,1},{2,10},{10... | collective-permute-start | bytes 196616 | tf_op jit(solution)/shard_map/ppermute | solution.py:690
  90.4 7.1 %collective-permute-done.8.refs_9_ = f32[8,2048]{1,0:T(8,128)S(1)} collective-permute-done((f32[8,2048]{1,0:T(8,128)S(1)}, f32[8,2048]{1,0:T(8,128)S(1)}, u32[]{:S(2)}, u32[]{:S(2)}) %collective-permute-start.8) | collective-permute-done | bytes 65568 | tf_op jit(solution)/shard_map/ppermute | solution.py:690
  97.5 0.1 gather.1
  97.5 0.8 copy.8
  (4 shorter events, 0.0 us)
Async XLA Ops:
  33.4 2.5 %collective-permute-start = (f32[4,72,512]{2,1,0:T(8,128)S(1)}, f32[4,72,512]{2,1,0:T(8,128)S(1)}, u32[]{:S(2)}, u32[]{:S(2)}) collective-permute-start(f32[4,72,512]{2,1,0:T(8,128)S(1)} %bitcast.3), channel_id=1, source_target_pairs={{0,1},{1,0},{2,3},{3,2},{4,5},{5,4},{6,7},{7,6},{8,9},{9,8},{10,11... | collective-permute-start | bytes 1769480 | tf_op jit(solution)/shard_map/ppermute | solution.py:626
  36.0 11.4 %copy-start = (f32[2,4,2048]{2,1,0:T(4,128)S(1)}, f32[2,4,2048]{2,1,0:T(4,128)}, u32[]{:S(2)}) copy-start(f32[2,4,2048]{2,1,0:T(4,128)} %refs_4_.7) | copy-start | bytes 196612
  36.0 11.4 %copy-start.1 = (s32[4,2048]{1,0:T(4,128)S(1)}, s32[4,2048]{1,0:T(4,128)}, u32[]{:S(2)}) copy-start(s32[4,2048]{1,0:T(4,128)} %refs_3_.7) | copy-start | bytes 98308
  51.4 8.1 %collective-permute-start.1 = (f32[4,2048]{1,0:T(4,128)S(1)}, f32[4,2048]{1,0:T(4,128)S(1)}, u32[]{:S(2)}, u32[]{:S(2)}) collective-permute-start(f32[4,2048]{1,0:T(4,128)S(1)} %get-tuple-element.37.refs_0_), channel_id=1, source_target_pairs={{0,8},{8,16},{16,24},{24,0},{1,9},{9,17},{17,25},{25,1},{2,10},{10... | collective-permute-start | bytes 98312 | tf_op jit(solution)/shard_map/ppermute | solution.py:687
  63.7 7.1 %collective-permute-start.3 = (f32[8,2048]{1,0:T(8,128)S(1)}, f32[8,2048]{1,0:T(8,128)S(1)}, u32[]{:S(2)}, u32[]{:S(2)}) collective-permute-start(f32[8,2048]{1,0:T(8,128)S(1)} %get-tuple-element.41.refs_5_), channel_id=1, source_target_pairs={{0,8},{8,16},{16,24},{24,0},{1,9},{9,17},{17,25},{25,1},{2,10},{10... | collective-permute-start | bytes 196616 | tf_op jit(solution)/shard_map/ppermute | solution.py:690
  63.8 7.0 %collective-permute-start.2 = (f32[4,2048]{1,0:T(4,128)S(1)}, f32[4,2048]{1,0:T(4,128)S(1)}, u32[]{:S(2)}, u32[]{:S(2)}) collective-permute-start(f32[4,2048]{1,0:T(4,128)S(1)} %get-tuple-element.40.refs_1_), channel_id=1, source_target_pairs={{0,8},{8,16},{16,24},{24,0},{1,9},{9,17},{17,25},{25,1},{2,10},{10... | collective-permute-start | bytes 98312 | tf_op jit(solution)/shard_map/ppermute | solution.py:687
  70.9 8.7 %collective-permute-start.5 = (f32[8,2048]{1,0:T(8,128)S(1)}, f32[8,2048]{1,0:T(8,128)S(1)}, u32[]{:S(2)}, u32[]{:S(2)}) collective-permute-start(f32[8,2048]{1,0:T(8,128)S(1)} %get-tuple-element.44.refs_6_), channel_id=1, source_target_pairs={{0,8},{8,16},{16,24},{24,0},{1,9},{9,17},{17,25},{25,1},{2,10},{10... | collective-permute-start | bytes 196616 | tf_op jit(solution)/shard_map/ppermute | solution.py:690
  73.9 5.7 %collective-permute-start.4 = (f32[4,2048]{1,0:T(4,128)S(1)}, f32[4,2048]{1,0:T(4,128)S(1)}, u32[]{:S(2)}, u32[]{:S(2)}) collective-permute-start(f32[4,2048]{1,0:T(4,128)S(1)} %get-tuple-element.43.refs_2_), channel_id=1, source_target_pairs={{0,8},{8,16},{16,24},{24,0},{1,9},{9,17},{17,25},{25,1},{2,10},{10... | collective-permute-start | bytes 98312 | tf_op jit(solution)/shard_map/ppermute | solution.py:687
  79.7 8.1 %collective-permute-start.7 = (f32[8,2048]{1,0:T(8,128)S(1)}, f32[8,2048]{1,0:T(8,128)S(1)}, u32[]{:S(2)}, u32[]{:S(2)}) collective-permute-start(f32[8,2048]{1,0:T(8,128)S(1)} %get-tuple-element.47.refs_7_), channel_id=1, source_target_pairs={{0,8},{8,16},{16,24},{24,0},{1,9},{9,17},{17,25},{25,1},{2,10},{10... | collective-permute-start | bytes 196616 | tf_op jit(solution)/shard_map/ppermute | solution.py:690
  80.9 7.0 %collective-permute-start.6 = (f32[4,2048]{1,0:T(4,128)S(1)}, f32[4,2048]{1,0:T(4,128)S(1)}, u32[]{:S(2)}, u32[]{:S(2)}) collective-permute-start(f32[4,2048]{1,0:T(4,128)S(1)} %get-tuple-element.46.refs_3_), channel_id=1, source_target_pairs={{0,8},{8,16},{16,24},{24,0},{1,9},{9,17},{17,25},{25,1},{2,10},{10... | collective-permute-start | bytes 98312 | tf_op jit(solution)/shard_map/ppermute | solution.py:687
  88.0 9.5 %collective-permute-start.8 = (f32[8,2048]{1,0:T(8,128)S(1)}, f32[8,2048]{1,0:T(8,128)S(1)}, u32[]{:S(2)}, u32[]{:S(2)}) collective-permute-start(f32[8,2048]{1,0:T(8,128)S(1)} %get-tuple-element.50.refs_8_), channel_id=1, source_target_pairs={{0,8},{8,16},{16,24},{24,0},{1,9},{9,17},{17,25},{25,1},{2,10},{10... | collective-permute-start | bytes 196616 | tf_op jit(solution)/shard_map/ppermute | solution.py:690
